TPU v7x, 256 devices: a whole 4x4x8 slice. The times are simulated.
256 devices in a mesh: img: 32 (over z_lo, x, y), pix: 8 (over z_hi, core).
Axes of the slice: x: 4, y: 4, z: 8 (z_hi: 4, z_lo: 2; z = z_hi * 2 + z_lo), core: 2. Of those that a mesh axis runs over, the one named last changes fastest.
Arguments:
- images: bfloat16 [8192, 16384], P('img', 'pix'), may hold values from -100 to 100
- references: bfloat16 [1536, 16384], P('img', 'pix'), may hold values from -6 to 6
- cycle_mask: int32 [16384], P('pix'), may hold values from 0 to 1, as said below
- view_class: int32 [1536], replicated, may hold values from 0 to 95, as said below
Outputs:
- view_sums: float32 [1536, 16384], P('img', 'pix')
- class_share: float32 [96], replicated
- image_evidence: float32 [8192], P(('img', 'pix'))
Inputs may be any that keep to these rules, and one draw needn't show every extreme that they name: `cycle_mask`: only pixels whose distance from the image centre lies between an inner radius and 64 are 1; some of them are left out as defective, never those in even columns, so the cycle is never empty. `view_class`: every class is named by exactly 16 views.
All inputs are finite; a program needn't handle non-finite values.
Results may differ from a plain program's by a relative error of at most 0.0023.
Values may be sent and summed in bfloat16 or wider, within the bound.
No kernel may reach another device: no remote copies, remote signals or barrier semaphores. Data moves between devices by JAX's collectives and lax.ppermute only.
A program may use at most 64 MiB of HBM per device.

v0:
```python
import jax
import jax.numpy as jnp
from jax import lax
from jax.sharding import Mesh, PartitionSpec as P

SIDE = 128
NCLS = 96
EPSILON = 1e-05
BF16, F32 = jnp.bfloat16, jnp.float32
PAIR = [(0, 1), (1, 0)]
FAR = [(zh, 4 + (zh - 1) % 4) for zh in range(4)] + [(4 + zh, (zh + 1) % 4) for zh in range(4)]


def place(zl, x, y):
    return zl * 16 + x * 4 + y


def plane(cross, step, first):
    pairs = []
    for zl in range(2):
        for x in range(4):
            for y in range(4):
                block = zl if first else zl ^ cross
                along_x = (block == 0) == first
                to = ((x - step) % 4, y) if along_x else (x, (y - step) % 4)
                pairs.append((place(zl, x, y), place(zl ^ cross if first else zl, *to)))
    return pairs


def ring_order(slots, position):
    return [
        lax.select_n(position, *[slots[(place - p) % 4] for p in range(4)]) for place in range(4)
    ]


def spread_sum(value, axes, count):
    sent = jnp.broadcast_to(value[None], (count,) + value.shape)
    return jnp.sum(lax.all_to_all(sent, axes, split_axis=0, concat_axis=0), 0)


def on_device(images, references, cycle_mask, view_class):
    zl, x, y, core = (lax.axis_index(a) for a in ("zl", "x", "y", "c"))
    rows, wide = images.shape
    half = wide // 2
    views = references.shape[0]
    total_images = rows * 32
    img = ("zl", "x", "y")
    mine = lambda a, axis: lax.dynamic_slice_in_dim(a, zl * half, half, axis)
    theirs = lambda a, axis: lax.dynamic_slice_in_dim(a, (1 - zl) * half, half, axis)
    swap = lambda a: lax.ppermute(a, "zl", PAIR)
    far = lambda a: lax.ppermute(a, ("zl", "zh"), FAR)

    widened = images.astype(F32)
    local = jnp.stack([jnp.sum(widened, 0), jnp.sum(widened * widened, 0)])
    moments = mine(local, 1) + swap(theirs(local, 1))
    ref_own, ref_other = mine(references, 1), theirs(references, 1)
    same = [ref_own] + [lax.ppermute(ref_own, img, plane(0, s, True)) for s in (1, 2, 3)]
    cross = [lax.ppermute(ref_other, img, plane(1, s, True)) for s in (0, 1, 2, 3)]
    img_other = swap(theirs(images, 1))
    img_own = mine(images, 1)
    moments = spread_sum(moments, ("x", "y"), 16)

    near = jnp.where(zl == 0, x, y)
    side = jnp.where(zl == 0, y, x)
    same = jnp.stack(ring_order(same, near))
    cross = jnp.stack(ring_order(cross, side))
    same2 = [same] + [lax.ppermute(same, img, plane(0, s, False)) for s in (1, 2, 3)]
    cross2 = [cross] + [lax.ppermute(cross, img, plane(1, s, False)) for s in (1, 2, 3)]

    shape = (4, 2, 32, half)
    own, other = img_own.reshape(shape), img_other.reshape(shape)
    pair = jnp.where(zl == 0, jnp.stack([own, other]), jnp.stack([other, own]))
    even, odd = pair[:, :, 0], pair[:, :, 1]
    block = jnp.where(core == 0, jnp.stack([even, odd]), jnp.stack([odd, even]))
    block = block.reshape(2 * rows, half)

    pix_mean = moments[0] / total_images
    pix_std = jnp.sqrt(moments[1] / total_images - pix_mean * pix_mean + EPSILON)
    whitened = (block.astype(F32) - pix_mean) / pix_std
    weight = mine(cycle_mask, 0).astype(F32)
    sums = jnp.stack([jnp.sum(whitened * weight, 1), jnp.sum(whitened * whitened * weight, 1)])
    sums = sums.reshape(2, 2, rows)
    sums = jnp.where(core == 0, sums, sums[:, ::-1])
    count = jnp.broadcast_to(jnp.sum(weight), (1, 2, rows))
    totals = spread_sum(jnp.concatenate([sums, count]).reshape(3, 2 * rows), ("zl", "zh", "c"), 16)
    totals = totals.reshape(3, 2, rows)
    totals = jnp.where(core == 0, totals, totals[:, ::-1]).reshape(3, 2 * rows)
    bg_mean = totals[0] / totals[2]
    bg_std = jnp.sqrt(totals[1] / totals[2] - bg_mean * bg_mean + EPSILON)
    normed = ((whitened - bg_mean[:, None]) / bg_std[:, None]).astype(BF16)

    same2, cross2 = ring_order(same2, side), ring_order(cross2, near)
    a = jnp.where(zl == 0, jnp.stack(same2, 1), jnp.stack(cross2, 1))
    b = jnp.where(zl == 0, jnp.stack(cross2), jnp.stack(same2))
    refs = jnp.stack([a, b]).reshape(32 * views, half)

    ref_energy = jnp.sum(jnp.square(refs.astype(F32)), 1)
    score = lambda a: (
        lax.dot_general(a, refs, (((1,), (1,)), ((), ())), preferred_element_type=F32)
        - 0.5 * ref_energy[None, :]
    )
    both = lax.ppermute(score(normed[rows:]), "c", PAIR)
    both = both + score(normed[:rows])
    both = both.reshape(2, rows // 2, 32 * views)
    cut = 16 * views
    kept = lax.dynamic_index_in_dim(both, zl, 0, False)
    sent = lax.dynamic_index_in_dim(both, 1 - zl, 0, False)
    kept = kept + jnp.concatenate([swap(sent[:, :cut]), far(sent[:, cut:])], 1)
    pieces = lax.all_to_all(kept.reshape(4, 32, -1), "zh", split_axis=0, concat_axis=0)
    scores = jnp.sum(pieces, 0) * (4.0 / SIDE)

    row_max = jnp.max(scores, 1, keepdims=True)
    log_total = row_max[:, 0] + jnp.log(jnp.sum(jnp.exp(scores - row_max), 1))
    evidence = log_total - jnp.mean(scores, 1)
    posterior = jnp.exp(scores - log_total[:, None]).astype(BF16)

    spread = jnp.broadcast_to(posterior[None], (4,) + posterior.shape)
    strip = lax.all_to_all(spread, "zh", split_axis=0, concat_axis=0).reshape(rows // 2, -1)
    class_mass = jnp.sum(strip, 0, dtype=F32)
    onehot = (view_class[:, None] == jnp.arange(NCLS, dtype=jnp.int32)[None, :]).astype(F32)
    share = jnp.dot(class_mass[None], onehot, precision=lax.Precision.HIGHEST)
    around = lambda a, axis: a + sum(
        lax.ppermute(a, axis, [(i, (i + s) % 4) for i in range(4)]) for s in (1, 2, 3)
    )
    share = around(share, "x")
    other_strip = [swap(strip[:, :cut]), far(strip[:, cut:])]
    other_strip = jnp.concatenate(other_strip, 1)
    gathered = jnp.where(
        zl == 0, jnp.concatenate([strip, other_strip]), jnp.concatenate([other_strip, strip])
    )
    gathered_c = lax.ppermute(gathered, "c", PAIR)
    gathered = jnp.concatenate([gathered, gathered_c])
    share = around(share, "y")
    share = share + swap(share)
    share = share + lax.ppermute(share, "c", PAIR)

    part = lax.dot_general(gathered, normed, (((0,), (0,)), ((), ())), preferred_element_type=F32)
    part = part.astype(BF16).reshape(32, views, half)
    part = lax.all_to_all(part, img, split_axis=0, concat_axis=0)
    part = jnp.sum(part.reshape(2, 16, views, half).astype(F32), 1)
    view_sums = jnp.concatenate([part[0], part[1]], 1)
    return (view_sums, share[0] * (NCLS / total_images), evidence)


def solution(mesh):
    fine = Mesh(mesh.devices.reshape(2, 4, 4, 4, 2), ("zl", "x", "y", "zh", "c"))
    img, pix = ("zl", "x", "y"), ("zh", "c")
    in_specs = (P(img, pix), P(img, pix), P(pix), P())
    out_specs = (P(img, pix), P(), P(img + pix))

    return jax.shard_map(
        on_device, mesh=fine, in_specs=in_specs, out_specs=out_specs, check_vma=False
    )
```

profile of v0, /device:TPU:1, one launch (start us, length us, event | category | flops | bytes accessed | tf_op | source)
XLA Modules:
  0.0 224.1 jit_solution(13466530247294558051)
XLA Ops:
  1.7 3.4 %collective-permute-start.4 = (bf16[48,1024]{1,0:T(8,128)(2,1)S(1)}, bf16[48,1024]{1,0:T(8,128)(2,1)S(1)}, u32[]{:S(2)}, u32[]{:S(2)}) collective-permute-start(bf16[48,1024]{1,0:T(8,128)(2,1)S(1)} %get-tuple-element.39), channel_id=1, source_target_pairs={{0,96},{8,104},{16,112},{24,120},{32,0},{40,8},{48,16},{56,24},{64... | collective-permute-start | bytes 294920 | tf_op jit(solution)/shard_map/ppermute | solution.py:57
  13.7 3.3 %collective-permute-start.10 = (bf16[48,1024]{1,0:T(8,128)(2,1)S(1)}, bf16[48,1024]{1,0:T(8,128)(2,1)S(1)}, u32[]{:S(2)}, u32[]{:S(2)}) collective-permute-start(bf16[48,1024]{1,0:T(8,128)(2,1)S(1)} %get-tuple-element.40), channel_id=1, source_target_pairs={{0,192},{8,200},{16,208},{24,216},{32,224},{40,232},{48,240},{56,2... | collective-permute-start | bytes 294920 | tf_op jit(solution)/shard_map/ppermute | solution.py:58
  17.8 3.5 %all-to-all-start = ((f32[16,2,1024]{2,1,0:T(2,128)}), f32[16,2,1024]{2,1,0:T(2,128)S(1)}, u32[]{:S(2)}, u32[]{:S(2)}) async-start(f32[16,2,1024]{2,1,0:T(2,128)} %broadcast_in_dim.8), calls=%async_computation | async-start | bytes 262144 | tf_op jit(solution)/shard_map/all_to_all | solution.py:38
  24.1 2.8 %collective-permute-start.6 = (bf16[4,48,1024]{2,1,0:T(8,128)(2,1)S(1)}, bf16[4,48,1024]{2,1,0:T(8,128)(2,1)S(1)}, u32[]{:S(2)}, u32[]{:S(2)}) collective-permute-start(bf16[4,48,1024]{2,1,0:T(8,128)(2,1)S(1)} %pad_maximum_fusion.1), channel_id=1, source_target_pairs={{0,16},{8,24},{16,0},{24,8},{32,48},{40,56},{48,32},{56,40},{64,80... | collective-permute-start | bytes 1179656 | tf_op jit(solution)/shard_map/ppermute | solution.py:67
  28.4 2.5 %collective-permute-start.13 = (bf16[4,48,1024]{2,1,0:T(8,128)(2,1)S(1)}, bf16[4,48,1024]{2,1,0:T(8,128)(2,1)S(1)}, u32[]{:S(2)}, u32[]{:S(2)}) collective-permute-start(bf16[4,48,1024]{2,1,0:T(8,128)(2,1)S(1)} %pad_maximum_fusion.2), channel_id=1, source_target_pairs={{0,64},{8,72},{16,80},{24,88},{32,96},{40,104},{48,112},{56,120},{... | collective-permute-start | bytes 1179656 | tf_op jit(solution)/shard_map/ppermute | solution.py:68
  31.1 5.7 %collective-permute-done.6 = bf16[4,48,1024]{2,1,0:T(8,128)(2,1)S(1)} collective-permute-done((bf16[4,48,1024]{2,1,0:T(8,128)(2,1)S(1)}, bf16[4,48,1024]{2,1,0:T(8,128)(2,1)S(1)}, u32[]{:S(2)}, u32[]{:S(2)}) %collective-permute-start.6) | collective-permute-done | bytes 393248 | tf_op jit(solution)/shard_map/ppermute | solution.py:67
  38.8 5.7 %collective-permute-done.7 = bf16[4,48,1024]{2,1,0:T(8,128)(2,1)S(1)} collective-permute-done((bf16[4,48,1024]{2,1,0:T(8,128)(2,1)S(1)}, bf16[4,48,1024]{2,1,0:T(8,128)(2,1)S(1)}, u32[]{:S(2)}, u32[]{:S(2)}) %collective-permute-start.7) | collective-permute-done | bytes 393248 | tf_op jit(solution)/shard_map/ppermute | solution.py:67
  47.9 6.9 %collective-permute-done.12 = bf16[4,48,1024]{2,1,0:T(8,128)(2,1)S(1)} collective-permute-done((bf16[4,48,1024]{2,1,0:T(8,128)(2,1)S(1)}, bf16[4,48,1024]{2,1,0:T(8,128)(2,1)S(1)}, u32[]{:S(2)}, u32[]{:S(2)}) %collective-permute-start.12) | collective-permute-done | bytes 393248 | tf_op jit(solution)/shard_map/ppermute | solution.py:68
  61.6 10.7 %all-to-all-start.1 = ((f32[16,3,512]{2,1,0:T(4,128)}), f32[16,3,512]{2,1,0:T(4,128)S(1)}, u32[]{:S(2)}, u32[]{:S(2)}) async-start(f32[16,3,512]{2,1,0:T(4,128)} %broadcast_in_dim.10), calls=%async_computation.1 | async-start | bytes 262144 | tf_op jit(solution)/shard_map/all_to_all | solution.py:38
  74.3 3.2 %fusion.9 = f32[2,2,4,32,1024]{4,3,2,1,0:T(8,128)} fusion(bf16[1,2,4,32,1024]{4,3,2,1,0:T(8,128)(2,1)} %copy-done.2, bf16[1,2,4,32,1024]{4,3,2,1,0:T(8,128)(2,1)} %copy-done.1, pred[]{:T(512)S(6)} %eq.11), kind=kLoop, calls=%fused_computation.25 | loop fusion | flops 2097152 | bytes 3145729 | tf_op jit(solution)/shard_map/convert_element_type | solution.py:79
  77.5 4.0 %all-to-all-done.1 = f32[16,3,512]{2,1,0:T(4,128)S(1)} async-done(((f32[16,3,512]{2,1,0:T(4,128)}), f32[16,3,512]{2,1,0:T(4,128)S(1)}, u32[]{:S(2)}, u32[]{:S(2)}) %all-to-all-start.1) | async-done | bytes 98336 | tf_op jit(solution)/shard_map/all_to_all | solution.py:38
  86.4 3.7 %collective-permute-done.15 = f32[256,1536]{1,0:T(8,128)} collective-permute-done((f32[256,1536]{1,0:T(8,128)}, f32[256,1536]{1,0:T(8,128)}, u32[]{:S(2)}, u32[]{:S(2)}) %collective-permute-start.15) | collective-permute-done | bytes 1572896 | tf_op jit(solution)/shard_map/ppermute | solution.py:102
  90.1 2.6 %fusion = f32[256,1536]{1,0:T(8,128)S(1)} fusion(f32[256,1536]{1,0:T(8,128)} %collective-permute-done.15, bf16[1536,1024]{1,0:T(8,128)(2,1)S(1)} %bitcast.97, f32[1536]{0:T(1024)S(1)} %mul.86, bf16[512,1024]{1,0:T(8,128)(2,1)} %copy-done.4), kind=kOutput, calls=%fused_computation.6 | convolution fusion | flops 806092800 | bytes 6821888 | tf_op jit(solution)/shard_map/dot_general | solution.py:99
  94.0 9.6 %collective-permute-done.16 = f32[128,768]{1,0:T(8,128)S(1)} collective-permute-done((f32[128,768]{1,0:T(8,128)S(1)}, f32[128,768]{1,0:T(8,128)S(1)}, u32[]{:S(2)}, u32[]{:S(2)}) %collective-permute-start.16) | collective-permute-done | bytes 393248 | tf_op jit(solution)/shard_map/ppermute | solution.py:50
  104.7 22.9 %all_to_all.25 = f32[4,32,1536]{2,1,0:T(8,128)S(1)} all-to-all(f32[4,32,1536]{2,1,0:T(8,128)S(1)} %maximum_add_fusion), channel_id=1, replica_groups=mesh['zl'=2,'x'=4,'y'=4,'zh'=4,'c'=2] {'zh'}, dimensions={0} | all-to-all | bytes 1572864 | tf_op jit(solution)/shard_map/all_to_all | solution.py:109
  128.7 14.9 %all_to_all.26 = bf16[4,32,1536]{2,1,0:T(8,128)(2,1)S(1)} all-to-all(bf16[4,32,1536]{2,1,0:T(8,128)(2,1)S(1)} %broadcast_in_dim.11), channel_id=1, replica_groups=mesh['zl'=2,'x'=4,'y'=4,'zh'=4,'c'=2] {'zh'}, dimensions={0} | all-to-all | bytes 786432 | tf_op jit(solution)/shard_map/all_to_all | solution.py:118
  143.7 3.1 %collective-permute-start.19 = (bf16[128,768]{1,0:T(8,128)(2,1)S(1)}, bf16[128,768]{1,0:T(8,128)(2,1)S(1)}, u32[]{:S(2)}, u32[]{:S(2)}) collective-permute-start(bf16[128,768]{1,0:T(8,128)(2,1)S(1)} %get-tuple-element.29), channel_id=1, source_target_pairs={{0,134},{2,128},{4,130},{6,132},{128,2},{130,4},{132,6},{134,0},{1... | collective-permute-start | bytes 589832 | tf_op jit(solution)/shard_map/ppermute | solution.py:51
  150.1 4.2 %collective-permute-start.20 = (bf16[256,1536]{1,0:T(8,128)(2,1)S(1)}, bf16[256,1536]{1,0:T(8,128)(2,1)S(1)}, u32[]{:S(2)}, u32[]{:S(2)}) collective-permute-start(bf16[256,1536]{1,0:T(8,128)(2,1)S(1)} %maximum_select_fusion.4), channel_id=1, source_target_pairs={{0,1},{1,0},{2,3},{3,2},{4,5},{5,4},{6,7},{7,6},{8,9},{9,8},{10,11... | collective-permute-start | bytes 2359304 | tf_op jit(solution)/shard_map/ppermute | solution.py:131
  156.2 3.5 %convolution_convert_fusion = bf16[1536,1024]{1,0:T(8,128)(2,1)} fusion(bf16[512,1024]{1,0:T(8,128)(2,1)S(1)} %copy-done.5, bf16[256,1536]{1,0:T(8,128)(2,1)S(1)} %collective-permute-done.20, bf16[256,1536]{1,0:T(8,128)(2,1)S(1)} %maximum_select_fusion.4), kind=kOutput, calls=%fused_computation.2 | convolution fusion | flops 1615331328 | bytes 5767168 | tf_op jit(solution)/shard_map/dot_general | solution.py:137
  159.7 6.1 %all-to-all-start.4 = ((bf16[32,48,1024]{2,1,0:T(8,128)(2,1)}), bf16[32,48,1024]{2,1,0:T(8,128)(2,1)S(1)}, u32[]{:S(2)}, u32[]{:S(2)}) async-start(bf16[32,48,1024]{2,1,0:T(8,128)(2,1)} %bitcast.117), calls=%async_computation.4 | async-start | bytes 6291456 | tf_op jit(solution)/shard_map/all_to_all | solution.py:139
  170.1 31.3 %collective-permute-done.23 = f32[1,96]{1,0:T(1,128)S(1)} collective-permute-done((f32[1,96]{1,0:T(1,128)S(1)}, f32[1,96]{1,0:T(1,128)S(1)}, u32[]{:S(2)}, u32[]{:S(2)}) %collective-permute-start.23) | collective-permute-done | bytes 416 | tf_op jit(solution)/shard_map/ppermute | solution.py:123
  202.2 3.9 %collective-permute-start.26 = (f32[1,96]{1,0:T(1,128)S(1)}, f32[1,96]{1,0:T(1,128)S(1)}, u32[]{:S(2)}, u32[]{:S(2)}) collective-permute-start(f32[1,96]{1,0:T(1,128)S(1)} %add_add_fusion.1), channel_id=1, source_target_pairs={{0,24},{8,0},{16,8},{24,16},{1,25},{9,1},{17,9},{25,17},{2,26},{10... | collective-permute-start | bytes 1160 | tf_op jit(solution)/shard_map/ppermute | solution.py:123
  211.5 4.5 %collective-permute-start.27 = (f32[1,96]{1,0:T(1,128)S(1)}, f32[1,96]{1,0:T(1,128)S(1)}, u32[]{:S(2)}, u32[]{:S(2)}) collective-permute-start(f32[1,96]{1,0:T(1,128)S(1)} %add_add_fusion), channel_id=1, source_target_pairs={{0,128},{128,0},{1,129},{129,1},{2,130},{130,2},{3,131},{131,3},{4... | collective-permute-start | bytes 1160 | tf_op jit(solution)/shard_map/ppermute | solution.py:50
  217.0 4.3 %collective-permute-start.28 = (f32[1,96]{1,0:T(1,128)S(1)}, f32[1,96]{1,0:T(1,128)S(1)}, u32[]{:S(2)}, u32[]{:S(2)}) collective-permute-start(f32[1,96]{1,0:T(1,128)S(1)} %add.97), channel_id=1, source_target_pairs={{0,1},{1,0},{2,3},{3,2},{4,5},{5,4},{6,7},{7,6},{8,9},{9,8},{10,11... | collective-permute-start | bytes 1160 | tf_op jit(solution)/shard_map/ppermute | solution.py:135
  (131 shorter events, 56.8 us)
Async XLA Ops:
  1.7 19.6 %collective-permute-start.4 = (bf16[48,1024]{1,0:T(8,128)(2,1)S(1)}, bf16[48,1024]{1,0:T(8,128)(2,1)S(1)}, u32[]{:S(2)}, u32[]{:S(2)}) collective-permute-start(bf16[48,1024]{1,0:T(8,128)(2,1)S(1)} %get-tuple-element.39), channel_id=1, source_target_pairs={{0,96},{8,104},{16,112},{24,120},{32,0},{40,8},{48,16},{56,24},{64... | collective-permute-start | bytes 294920 | tf_op jit(solution)/shard_map/ppermute | solution.py:57
  5.1 17.4 %collective-permute-start.3 = (bf16[48,1024]{1,0:T(8,128)(2,1)S(1)}, bf16[48,1024]{1,0:T(8,128)(2,1)S(1)}, u32[]{:S(2)}, u32[]{:S(2)}) collective-permute-start(bf16[48,1024]{1,0:T(8,128)(2,1)S(1)} %get-tuple-element.39), channel_id=1, source_target_pairs={{0,64},{8,72},{16,80},{24,88},{32,96},{40,104},{48,112},{56,120},{... | collective-permute-start | bytes 294920 | tf_op jit(solution)/shard_map/ppermute | solution.py:57
  5.6 18.2 %collective-permute-start.2 = (bf16[48,1024]{1,0:T(8,128)(2,1)S(1)}, bf16[48,1024]{1,0:T(8,128)(2,1)S(1)}, u32[]{:S(2)}, u32[]{:S(2)}) collective-permute-start(bf16[48,1024]{1,0:T(8,128)(2,1)S(1)} %get-tuple-element.39), channel_id=1, source_target_pairs={{0,32},{8,40},{16,48},{24,56},{32,64},{40,72},{48,80},{56,88},{64,... | collective-permute-start | bytes 294920 | tf_op jit(solution)/shard_map/ppermute | solution.py:57
  9.7 14.3 %collective-permute-start.11 = (bf16[48,1024]{1,0:T(8,128)(2,1)S(1)}, bf16[48,1024]{1,0:T(8,128)(2,1)S(1)}, u32[]{:S(2)}, u32[]{:S(2)}) collective-permute-start(bf16[48,1024]{1,0:T(8,128)(2,1)S(1)} %get-tuple-element.40), channel_id=1, source_target_pairs={{0,224},{8,232},{16,240},{24,248},{32,128},{40,136},{48,144},{56,1... | collective-permute-start | bytes 294920 | tf_op jit(solution)/shard_map/ppermute | solution.py:58
  13.7 13.2 %collective-permute-start.10 = (bf16[48,1024]{1,0:T(8,128)(2,1)S(1)}, bf16[48,1024]{1,0:T(8,128)(2,1)S(1)}, u32[]{:S(2)}, u32[]{:S(2)}) collective-permute-start(bf16[48,1024]{1,0:T(8,128)(2,1)S(1)} %get-tuple-element.40), channel_id=1, source_target_pairs={{0,192},{8,200},{16,208},{24,216},{32,224},{40,232},{48,240},{56,2... | collective-permute-start | bytes 294920 | tf_op jit(solution)/shard_map/ppermute | solution.py:58
  17.8 13.2 %all-to-all-start = ((f32[16,2,1024]{2,1,0:T(2,128)}), f32[16,2,1024]{2,1,0:T(2,128)S(1)}, u32[]{:S(2)}, u32[]{:S(2)}) async-start(f32[16,2,1024]{2,1,0:T(2,128)} %broadcast_in_dim.8), calls=%async_computation | async-start | bytes 262144 | tf_op jit(solution)/shard_map/all_to_all | solution.py:38
  21.3 6.4 %collective-permute-start.9 = (bf16[48,1024]{1,0:T(8,128)(2,1)S(1)}, bf16[48,1024]{1,0:T(8,128)(2,1)S(1)}, u32[]{:S(2)}, u32[]{:S(2)}) collective-permute-start(bf16[48,1024]{1,0:T(8,128)(2,1)S(1)} %get-tuple-element.40), channel_id=1, source_target_pairs={{0,160},{8,168},{16,176},{24,184},{32,192},{40,200},{48,208},{56,2... | collective-permute-start | bytes 294920 | tf_op jit(solution)/shard_map/ppermute | solution.py:58
  23.8 32.7 %collective-permute-start = (bf16[256,1024]{1,0:T(8,128)(2,1)}, bf16[256,1024]{1,0:T(8,128)(2,1)}, u32[]{:S(2)}, u32[]{:S(2)}) collective-permute-start(bf16[256,1024]{1,0:T(8,128)(2,1)} %get-tuple-element.24), channel_id=1, source_target_pairs={{0,128},{128,0},{1,129},{129,1},{2,130},{130,2},{3,131},{131,3},{4... | collective-permute-start | bytes 1572872 | tf_op jit(solution)/shard_map/ppermute | solution.py:50
  24.1 12.7 %collective-permute-start.6 = (bf16[4,48,1024]{2,1,0:T(8,128)(2,1)S(1)}, bf16[4,48,1024]{2,1,0:T(8,128)(2,1)S(1)}, u32[]{:S(2)}, u32[]{:S(2)}) collective-permute-start(bf16[4,48,1024]{2,1,0:T(8,128)(2,1)S(1)} %pad_maximum_fusion.1), channel_id=1, source_target_pairs={{0,16},{8,24},{16,0},{24,8},{32,48},{40,56},{48,32},{56,40},{64,80... | collective-permute-start | bytes 1179656 | tf_op jit(solution)/shard_map/ppermute | solution.py:67
  26.8 17.6 %collective-permute-start.7 = (bf16[4,48,1024]{2,1,0:T(8,128)(2,1)S(1)}, bf16[4,48,1024]{2,1,0:T(8,128)(2,1)S(1)}, u32[]{:S(2)}, u32[]{:S(2)}) collective-permute-start(bf16[4,48,1024]{2,1,0:T(8,128)(2,1)S(1)} %pad_maximum_fusion.1), channel_id=1, source_target_pairs={{0,24},{8,0},{16,8},{24,16},{32,56},{40,32},{48,40},{56,48},{64,88... | collective-permute-start | bytes 1179656 | tf_op jit(solution)/shard_map/ppermute | solution.py:67
  27.7 19.3 %collective-permute-start.5 = (bf16[4,48,1024]{2,1,0:T(8,128)(2,1)S(1)}, bf16[4,48,1024]{2,1,0:T(8,128)(2,1)S(1)}, u32[]{:S(2)}, u32[]{:S(2)}) collective-permute-start(bf16[4,48,1024]{2,1,0:T(8,128)(2,1)S(1)} %pad_maximum_fusion.1), channel_id=1, source_target_pairs={{0,8},{8,16},{16,24},{24,0},{32,40},{40,48},{48,56},{56,32},{64,72... | collective-permute-start | bytes 1179656 | tf_op jit(solution)/shard_map/ppermute | solution.py:67
  28.4 18.9 %collective-permute-start.13 = (bf16[4,48,1024]{2,1,0:T(8,128)(2,1)S(1)}, bf16[4,48,1024]{2,1,0:T(8,128)(2,1)S(1)}, u32[]{:S(2)}, u32[]{:S(2)}) collective-permute-start(bf16[4,48,1024]{2,1,0:T(8,128)(2,1)S(1)} %pad_maximum_fusion.2), channel_id=1, source_target_pairs={{0,64},{8,72},{16,80},{24,88},{32,96},{40,104},{48,112},{56,120},{... | collective-permute-start | bytes 1179656 | tf_op jit(solution)/shard_map/ppermute | solution.py:68
  36.7 11.1 %collective-permute-start.14 = (bf16[4,48,1024]{2,1,0:T(8,128)(2,1)S(1)}, bf16[4,48,1024]{2,1,0:T(8,128)(2,1)S(1)}, u32[]{:S(2)}, u32[]{:S(2)}) collective-permute-start(bf16[4,48,1024]{2,1,0:T(8,128)(2,1)S(1)} %pad_maximum_fusion.2), channel_id=1, source_target_pairs={{0,96},{8,104},{16,112},{24,120},{32,0},{40,8},{48,16},{56,24},{64... | collective-permute-start | bytes 1179656 | tf_op jit(solution)/shard_map/ppermute | solution.py:68
  44.5 10.3 %collective-permute-start.12 = (bf16[4,48,1024]{2,1,0:T(8,128)(2,1)S(1)}, bf16[4,48,1024]{2,1,0:T(8,128)(2,1)S(1)}, u32[]{:S(2)}, u32[]{:S(2)}) collective-permute-start(bf16[4,48,1024]{2,1,0:T(8,128)(2,1)S(1)} %pad_maximum_fusion.2), channel_id=1, source_target_pairs={{0,32},{8,40},{16,48},{24,56},{32,64},{40,72},{48,80},{56,88},{64,... | collective-permute-start | bytes 1179656 | tf_op jit(solution)/shard_map/ppermute | solution.py:68
  61.6 19.8 %all-to-all-start.1 = ((f32[16,3,512]{2,1,0:T(4,128)}), f32[16,3,512]{2,1,0:T(4,128)S(1)}, u32[]{:S(2)}, u32[]{:S(2)}) async-start(f32[16,3,512]{2,1,0:T(4,128)} %broadcast_in_dim.10), calls=%async_computation.1 | async-start | bytes 262144 | tf_op jit(solution)/shard_map/all_to_all | solution.py:38
  92.9 10.6 %collective-permute-start.16 = (f32[128,768]{1,0:T(8,128)S(1)}, f32[128,768]{1,0:T(8,128)S(1)}, u32[]{:S(2)}, u32[]{:S(2)}) collective-permute-start(f32[128,768]{1,0:T(8,128)S(1)} %get-tuple-element.25), channel_id=1, source_target_pairs={{0,128},{128,0},{1,129},{129,1},{2,130},{130,2},{3,131},{131,3},{4... | collective-permute-start | bytes 1179656 | tf_op jit(solution)/shard_map/ppermute | solution.py:50
  93.2 11.5 %collective-permute-start.17 = (f32[128,768]{1,0:T(8,128)S(1)}, f32[128,768]{1,0:T(8,128)S(1)}, u32[]{:S(2)}, u32[]{:S(2)}) collective-permute-start(f32[128,768]{1,0:T(8,128)S(1)} %get-tuple-element.26), channel_id=1, source_target_pairs={{0,134},{2,128},{4,130},{6,132},{128,2},{130,4},{132,6},{134,0},{1... | collective-permute-start | bytes 1179656 | tf_op jit(solution)/shard_map/ppermute | solution.py:51
  143.7 6.2 %collective-permute-start.19 = (bf16[128,768]{1,0:T(8,128)(2,1)S(1)}, bf16[128,768]{1,0:T(8,128)(2,1)S(1)}, u32[]{:S(2)}, u32[]{:S(2)}) collective-permute-start(bf16[128,768]{1,0:T(8,128)(2,1)S(1)} %get-tuple-element.29), channel_id=1, source_target_pairs={{0,134},{2,128},{4,130},{6,132},{128,2},{130,4},{132,6},{134,0},{1... | collective-permute-start | bytes 589832 | tf_op jit(solution)/shard_map/ppermute | solution.py:51
  150.1 6.1 %collective-permute-start.20 = (bf16[256,1536]{1,0:T(8,128)(2,1)S(1)}, bf16[256,1536]{1,0:T(8,128)(2,1)S(1)}, u32[]{:S(2)}, u32[]{:S(2)}) collective-permute-start(bf16[256,1536]{1,0:T(8,128)(2,1)S(1)} %maximum_select_fusion.4), channel_id=1, source_target_pairs={{0,1},{1,0},{2,3},{3,2},{4,5},{5,4},{6,7},{7,6},{8,9},{9,8},{10,11... | collective-permute-start | bytes 2359304 | tf_op jit(solution)/shard_map/ppermute | solution.py:131
  159.7 63.0 %all-to-all-start.4 = ((bf16[32,48,1024]{2,1,0:T(8,128)(2,1)}), bf16[32,48,1024]{2,1,0:T(8,128)(2,1)S(1)}, u32[]{:S(2)}, u32[]{:S(2)}) async-start(bf16[32,48,1024]{2,1,0:T(8,128)(2,1)} %bitcast.117), calls=%async_computation.4 | async-start | bytes 6291456 | tf_op jit(solution)/shard_map/all_to_all | solution.py:139
  166.4 35.0 %collective-permute-start.23 = (f32[1,96]{1,0:T(1,128)S(1)}, f32[1,96]{1,0:T(1,128)S(1)}, u32[]{:S(2)}, u32[]{:S(2)}) collective-permute-start(f32[1,96]{1,0:T(1,128)S(1)} %fusion.10), channel_id=1, source_target_pairs={{0,96},{32,0},{64,32},{96,64},{1,97},{33,1},{65,33},{97,65},{2,98}... | collective-permute-start | bytes 1160 | tf_op jit(solution)/shard_map/ppermute | solution.py:123
  168.9 32.4 %collective-permute-start.22 = (f32[1,96]{1,0:T(1,128)S(1)}, f32[1,96]{1,0:T(1,128)S(1)}, u32[]{:S(2)}, u32[]{:S(2)}) collective-permute-start(f32[1,96]{1,0:T(1,128)S(1)} %fusion.10), channel_id=1, source_target_pairs={{0,64},{32,96},{64,0},{96,32},{1,65},{33,97},{65,1},{97,33},{2,66}... | collective-permute-start | bytes 1160 | tf_op jit(solution)/shard_map/ppermute | solution.py:123
  169.5 32.7 %collective-permute-start.21 = (f32[1,96]{1,0:T(1,128)S(1)}, f32[1,96]{1,0:T(1,128)S(1)}, u32[]{:S(2)}, u32[]{:S(2)}) collective-permute-start(f32[1,96]{1,0:T(1,128)S(1)} %fusion.10), channel_id=1, source_target_pairs={{0,32},{32,64},{64,96},{96,0},{1,33},{33,65},{65,97},{97,1},{2,34}... | collective-permute-start | bytes 1160 | tf_op jit(solution)/shard_map/ppermute | solution.py:123
  202.2 6.2 %collective-permute-start.26 = (f32[1,96]{1,0:T(1,128)S(1)}, f32[1,96]{1,0:T(1,128)S(1)}, u32[]{:S(2)}, u32[]{:S(2)}) collective-permute-start(f32[1,96]{1,0:T(1,128)S(1)} %add_add_fusion.1), channel_id=1, source_target_pairs={{0,24},{8,0},{16,8},{24,16},{1,25},{9,1},{17,9},{25,17},{2,26},{10... | collective-permute-start | bytes 1160 | tf_op jit(solution)/shard_map/ppermute | solution.py:123
  (17 other events, 88.4 us)
where the time goes:
time: 225 us; the launch traced here: 224 us
  waiting for transfers between devices  80.8 us (36%)
  starting transfers between devices  71.9 us (32%)
  blocking collectives  37.8 us (17%)
  other arithmetic  17.2 us (8%)
  matrix products  8.74 us (4%)
  local copies, waits for them, and re-layouts  6.51 us (3%)
    ppermute x6, waiting for transfers between devices, on_device(): lax.ppermute(a, axis, [(i, (i + s) % 4) for i in range(4)])  35.2 us
    all_to_all x1, blocking collectives, on_device(): lax.all_to_all(kept.reshape(4, 32, -1), 'zh', split_axis=0, concat_axis=0)  22.9 us
    all_to_all x1, blocking collectives, on_device(): lax.all_to_all(spread, 'zh', split_axis=0, concat_axis=0)  14.9 us
    all_to_all x2, starting transfers between devices, spread_sum(): return jnp.sum(lax.all_to_all(sent, axes, split_axis=0, concat_axis=0), 0)  14.2 us
    ppermute x3, waiting for transfers between devices, on_device(): lax.ppermute(same, img, plane(0, s, False))  13 us
    ppermute x5, waiting for transfers between devices, on_device(): swap = lambda a: lax.ppermute(a, 'zl', PAIR)  11.9 us
    ppermute x6, starting transfers between devices, on_device(): lax.ppermute(a, axis, [(i, (i + s) % 4) for i in range(4)])  9.91 us
    ppermute x4, starting transfers between devices, on_device(): lax.ppermute(ref_other, img, plane(1, s, True))  8.13 us
  transfers between devices with their start and end apart: 32, of which 18 were waited for; matrix products, arithmetic and copies ran while one was open for 6% of the time, Pallas kernels for 0%

commit v1 on v0

--- a/solution.py
+++ b/solution.py
@@ -33,9 +33,9 @@
     ]
 
 
-def spread_sum(value, axes, count):
+def spread(value, axes, count):
     sent = jnp.broadcast_to(value[None], (count,) + value.shape)
-    return jnp.sum(lax.all_to_all(sent, axes, split_axis=0, concat_axis=0), 0)
+    return lax.all_to_all(sent, axes, split_axis=0, concat_axis=0)
 
 
 def on_device(images, references, cycle_mask, view_class):
@@ -52,13 +52,14 @@
 
     widened = images.astype(F32)
     local = jnp.stack([jnp.sum(widened, 0), jnp.sum(widened * widened, 0)])
-    moments = mine(local, 1) + swap(theirs(local, 1))
+    moments = swap(theirs(local, 1))
+    moments = mine(local, 1) + moments
     ref_own, ref_other = mine(references, 1), theirs(references, 1)
     same = [ref_own] + [lax.ppermute(ref_own, img, plane(0, s, True)) for s in (1, 2, 3)]
     cross = [lax.ppermute(ref_other, img, plane(1, s, True)) for s in (0, 1, 2, 3)]
     img_other = swap(theirs(images, 1))
     img_own = mine(images, 1)
-    moments = spread_sum(moments, ("x", "y"), 16)
+    moments = jnp.sum(spread(moments, ("x", "y"), 16), 0)
 
     near = jnp.where(zl == 0, x, y)
     side = jnp.where(zl == 0, y, x)
@@ -82,7 +83,10 @@
     sums = sums.reshape(2, 2, rows)
     sums = jnp.where(core == 0, sums, sums[:, ::-1])
     count = jnp.broadcast_to(jnp.sum(weight), (1, 2, rows))
-    totals = spread_sum(jnp.concatenate([sums, count]).reshape(3, 2 * rows), ("zl", "zh", "c"), 16)
+    totals = spread(
+        jnp.concatenate([sums, count]).reshape(3, 2 * rows), ("zl", "zh", "c"), 16
+    )
+    totals = jnp.sum(totals, 0)
     totals = totals.reshape(3, 2, rows)
     totals = jnp.where(core == 0, totals, totals[:, ::-1]).reshape(3, 2 * rows)
     bg_mean = totals[0] / totals[2]
@@ -100,7 +104,7 @@
         - 0.5 * ref_energy[None, :]
     )
     both = lax.ppermute(score(normed[rows:]), "c", PAIR)
-    both = both + score(normed[:rows])
+    both = both + lax.optimization_barrier(score(normed[:rows]))
     both = both.reshape(2, rows // 2, 32 * views)
     cut = 16 * views
     kept = lax.dynamic_index_in_dim(both, zl, 0, False)
@@ -114,8 +118,7 @@
     evidence = log_total - jnp.mean(scores, 1)
     posterior = jnp.exp(scores - log_total[:, None]).astype(BF16)
 
-    spread = jnp.broadcast_to(posterior[None], (4,) + posterior.shape)
-    strip = lax.all_to_all(spread, "zh", split_axis=0, concat_axis=0).reshape(rows // 2, -1)
+    strip = spread(posterior, "zh", 4).reshape(rows // 2, -1)
     class_mass = jnp.sum(strip, 0, dtype=F32)
     onehot = (view_class[:, None] == jnp.arange(NCLS, dtype=jnp.int32)[None, :]).astype(F32)
     share = jnp.dot(class_mass[None], onehot, precision=lax.Precision.HIGHEST)

time: 225 us -> 224 us (level)
    ppermute x6, waiting for transfers between devices: 35.2 us -> 31.6 us  [on_device(): lax.ppermute(a, axis, [(i, (i + s) % 4) for i in range(4)])]
    ppermute x6, starting transfers between devices: 9.91 us -> 12.3 us  [on_device(): lax.ppermute(a, axis, [(i, (i + s) % 4) for i in range(4)])]
  transfers between devices with their start and end apart: 32 -> 32, of which waited for: 18 -> 17; matrix products, arithmetic and copies ran while one was open for 6% -> 6% of each run, Pallas kernels for 0% -> 0%
where the time goes in v1:
time: 224 us; the launch traced here: 223 us
  waiting for transfers between devices  78.8 us (35%)
  starting transfers between devices  73.6 us (33%)
  blocking collectives  38.1 us (17%)
  other arithmetic  15.7 us (7%)
  matrix products  8.18 us (4%)
  local copies, waits for them, and re-layouts  7.99 us (4%)
    ppermute x6, waiting for transfers between devices, on_device(): lax.ppermute(a, axis, [(i, (i + s) % 4) for i in range(4)])  31.6 us
    all_to_all x1, blocking collectives, on_device(): lax.all_to_all(kept.reshape(4, 32, -1), 'zh', split_axis=0, concat_axis=0)  22.9 us
    all_to_all x1, blocking collectives, spread(): return lax.all_to_all(sent, axes, split_axis=0, concat_axis=0)  15.2 us
    all_to_all x2, starting transfers between devices, spread(): return lax.all_to_all(sent, axes, split_axis=0, concat_axis=0)  15 us
    ppermute x5, waiting for transfers between devices, on_device(): swap = lambda a: lax.ppermute(a, 'zl', PAIR)  13 us
    ppermute x6, starting transfers between devices, on_device(): lax.ppermute(a, axis, [(i, (i + s) % 4) for i in range(4)])  12.3 us
    ppermute x3, waiting for transfers between devices, on_device(): lax.ppermute(same, img, plane(0, s, False))  12.2 us
    ppermute x3, waiting for transfers between devices, on_device(): lax.ppermute(cross, img, plane(1, s, False))  9.53 us
  transfers between devices with their start and end apart: 32, of which 17 were waited for; matrix products, arithmetic and copies ran while one was open for 6% of the time, Pallas kernels for 0%

profile of v1, /device:TPU:1, one launch (start us, length us, event | category | flops | bytes accessed | tf_op | source)
XLA Modules:
  0.0 223.4 jit_solution(11817637209211480979)
XLA Ops:
  1.7 2.1 collective-permute-start.2
  3.8 2.5 %collective-permute-start.3 = (bf16[48,1024]{1,0:T(8,128)(2,1)S(1)}, bf16[48,1024]{1,0:T(8,128)(2,1)S(1)}, u32[]{:S(2)}, u32[]{:S(2)}) collective-permute-start(bf16[48,1024]{1,0:T(8,128)(2,1)S(1)} %get-tuple-element.39), channel_id=1, source_target_pairs={{0,64},{8,72},{16,80},{24,88},{32,96},{40,104},{48,112},{56,120},{... | collective-permute-start | bytes 294920 | tf_op jit(solution)/shard_map/ppermute | solution.py:58
  7.4 4.3 %collective-permute-start.10 = (bf16[48,1024]{1,0:T(8,128)(2,1)S(1)}, bf16[48,1024]{1,0:T(8,128)(2,1)S(1)}, u32[]{:S(2)}, u32[]{:S(2)}) collective-permute-start(bf16[48,1024]{1,0:T(8,128)(2,1)S(1)} %get-tuple-element.40), channel_id=1, source_target_pairs={{0,192},{8,200},{16,208},{24,216},{32,224},{40,232},{48,240},{56,2... | collective-permute-start | bytes 294920 | tf_op jit(solution)/shard_map/ppermute | solution.py:59
  17.9 3.5 %all-to-all-start = ((f32[16,2,1024]{2,1,0:T(2,128)}), f32[16,2,1024]{2,1,0:T(2,128)S(1)}, u32[]{:S(2)}, u32[]{:S(2)}) async-start(f32[16,2,1024]{2,1,0:T(2,128)} %broadcast_in_dim.8), calls=%async_computation | async-start | bytes 262144 | tf_op jit(solution)/shard_map/all_to_all | solution.py:38
  30.8 5.0 %collective-permute-done.5 = bf16[4,48,1024]{2,1,0:T(8,128)(2,1)S(1)} collective-permute-done((bf16[4,48,1024]{2,1,0:T(8,128)(2,1)S(1)}, bf16[4,48,1024]{2,1,0:T(8,128)(2,1)S(1)}, u32[]{:S(2)}, u32[]{:S(2)}) %collective-permute-start.5) | collective-permute-done | bytes 393248 | tf_op jit(solution)/shard_map/ppermute | solution.py:68
  35.8 2.1 collective-permute-start.13
  37.9 7.2 %collective-permute-done.6 = bf16[4,48,1024]{2,1,0:T(8,128)(2,1)S(1)} collective-permute-done((bf16[4,48,1024]{2,1,0:T(8,128)(2,1)S(1)}, bf16[4,48,1024]{2,1,0:T(8,128)(2,1)S(1)}, u32[]{:S(2)}, u32[]{:S(2)}) %collective-permute-start.6) | collective-permute-done | bytes 393248 | tf_op jit(solution)/shard_map/ppermute | solution.py:68
  48.0 8.4 %collective-permute-done.14 = bf16[4,48,1024]{2,1,0:T(8,128)(2,1)S(1)} collective-permute-done((bf16[4,48,1024]{2,1,0:T(8,128)(2,1)S(1)}, bf16[4,48,1024]{2,1,0:T(8,128)(2,1)S(1)}, u32[]{:S(2)}, u32[]{:S(2)}) %collective-permute-start.14) | collective-permute-done | bytes 393248 | tf_op jit(solution)/shard_map/ppermute | solution.py:69
  63.2 11.5 %all-to-all-start.1 = ((f32[16,3,512]{2,1,0:T(4,128)}), f32[16,3,512]{2,1,0:T(4,128)S(1)}, u32[]{:S(2)}, u32[]{:S(2)}) async-start(f32[16,3,512]{2,1,0:T(4,128)} %broadcast_in_dim.10), calls=%async_computation.1 | async-start | bytes 262144 | tf_op jit(solution)/shard_map/all_to_all | solution.py:38
  78.5 5.4 %all-to-all-done.1 = f32[16,3,512]{2,1,0:T(4,128)S(1)} async-done(((f32[16,3,512]{2,1,0:T(4,128)}), f32[16,3,512]{2,1,0:T(4,128)S(1)}, u32[]{:S(2)}, u32[]{:S(2)}) %all-to-all-start.1) | async-done | bytes 98336 | tf_op jit(solution)/shard_map/all_to_all | solution.py:38
  86.4 2.2 convolution_subtract_fusion.1
  88.6 2.1 convolution_subtract_fusion
  95.2 9.6 %collective-permute-done.16 = f32[128,768]{1,0:T(8,128)S(1)} collective-permute-done((f32[128,768]{1,0:T(8,128)S(1)}, f32[128,768]{1,0:T(8,128)S(1)}, u32[]{:S(2)}, u32[]{:S(2)}) %collective-permute-start.16) | collective-permute-done | bytes 393248 | tf_op jit(solution)/shard_map/ppermute | solution.py:50
  106.0 22.9 %all_to_all.25 = f32[4,32,1536]{2,1,0:T(8,128)S(1)} all-to-all(f32[4,32,1536]{2,1,0:T(8,128)S(1)} %maximum_add_fusion), channel_id=1, replica_groups=mesh['zl'=2,'x'=4,'y'=4,'zh'=4,'c'=2] {'zh'}, dimensions={0} | all-to-all | bytes 1572864 | tf_op jit(solution)/shard_map/all_to_all | solution.py:113
  129.9 15.2 %all_to_all.26 = bf16[4,32,1536]{2,1,0:T(8,128)(2,1)S(1)} all-to-all(bf16[4,32,1536]{2,1,0:T(8,128)(2,1)S(1)} %broadcast_in_dim.11), channel_id=1, replica_groups=mesh['zl'=2,'x'=4,'y'=4,'zh'=4,'c'=2] {'zh'}, dimensions={0} | all-to-all | bytes 786432 | tf_op jit(solution)/shard_map/all_to_all | solution.py:38
  145.3 2.9 %collective-permute-start.19 = (bf16[128,768]{1,0:T(8,128)(2,1)S(1)}, bf16[128,768]{1,0:T(8,128)(2,1)S(1)}, u32[]{:S(2)}, u32[]{:S(2)}) collective-permute-start(bf16[128,768]{1,0:T(8,128)(2,1)S(1)} %get-tuple-element.29), channel_id=1, source_target_pairs={{0,134},{2,128},{4,130},{6,132},{128,2},{130,4},{132,6},{134,0},{1... | collective-permute-start | bytes 589832 | tf_op jit(solution)/shard_map/ppermute | solution.py:51
  151.4 4.4 %collective-permute-start.20 = (bf16[256,1536]{1,0:T(8,128)(2,1)S(1)}, bf16[256,1536]{1,0:T(8,128)(2,1)S(1)}, u32[]{:S(2)}, u32[]{:S(2)}) collective-permute-start(bf16[256,1536]{1,0:T(8,128)(2,1)S(1)} %maximum_select_fusion.4), channel_id=1, source_target_pairs={{0,1},{1,0},{2,3},{3,2},{4,5},{5,4},{6,7},{7,6},{8,9},{9,8},{10,11... | collective-permute-start | bytes 2359304 | tf_op jit(solution)/shard_map/ppermute | solution.py:134
  157.7 3.5 %convolution_convert_fusion = bf16[1536,1024]{1,0:T(8,128)(2,1)} fusion(bf16[512,1024]{1,0:T(8,128)(2,1)S(1)} %copy-done.7, bf16[256,1536]{1,0:T(8,128)(2,1)S(1)} %collective-permute-done.20, bf16[256,1536]{1,0:T(8,128)(2,1)S(1)} %maximum_select_fusion.4), kind=kOutput, calls=%fused_computation.2 | convolution fusion | flops 1615331328 | bytes 5767168 | tf_op jit(solution)/shard_map/dot_general | solution.py:140
  161.2 5.5 %all-to-all-start.4 = ((bf16[32,48,1024]{2,1,0:T(8,128)(2,1)}), bf16[32,48,1024]{2,1,0:T(8,128)(2,1)S(1)}, u32[]{:S(2)}, u32[]{:S(2)}) async-start(bf16[32,48,1024]{2,1,0:T(8,128)(2,1)} %bitcast.115), calls=%async_computation.4 | async-start | bytes 6291456 | tf_op jit(solution)/shard_map/all_to_all | solution.py:142
  168.6 2.4 %collective-permute-start.22 = (f32[1,96]{1,0:T(1,128)S(1)}, f32[1,96]{1,0:T(1,128)S(1)}, u32[]{:S(2)}, u32[]{:S(2)}) collective-permute-start(f32[1,96]{1,0:T(1,128)S(1)} %fusion.9), channel_id=1, source_target_pairs={{0,64},{32,96},{64,0},{96,32},{1,65},{33,97},{65,1},{97,33},{2,66}... | collective-permute-start | bytes 1160 | tf_op jit(solution)/shard_map/ppermute | solution.py:126
  172.2 30.9 %collective-permute-done.21 = f32[1,96]{1,0:T(1,128)S(1)} collective-permute-done((f32[1,96]{1,0:T(1,128)S(1)}, f32[1,96]{1,0:T(1,128)S(1)}, u32[]{:S(2)}, u32[]{:S(2)}) %collective-permute-start.21) | collective-permute-done | bytes 416 | tf_op jit(solution)/shard_map/ppermute | solution.py:126
  203.1 3.8 %collective-permute-start.24 = (f32[1,96]{1,0:T(1,128)S(1)}, f32[1,96]{1,0:T(1,128)S(1)}, u32[]{:S(2)}, u32[]{:S(2)}) collective-permute-start(f32[1,96]{1,0:T(1,128)S(1)} %add_add_fusion.1), channel_id=1, source_target_pairs={{0,8},{8,16},{16,24},{24,0},{1,9},{9,17},{17,25},{25,1},{2,10},{10... | collective-permute-start | bytes 1160 | tf_op jit(solution)/shard_map/ppermute | solution.py:126
  211.3 4.3 %collective-permute-start.27 = (f32[1,96]{1,0:T(1,128)S(1)}, f32[1,96]{1,0:T(1,128)S(1)}, u32[]{:S(2)}, u32[]{:S(2)}) collective-permute-start(f32[1,96]{1,0:T(1,128)S(1)} %add_add_fusion), channel_id=1, source_target_pairs={{0,128},{128,0},{1,129},{129,1},{2,130},{130,2},{3,131},{131,3},{4... | collective-permute-start | bytes 1160 | tf_op jit(solution)/shard_map/ppermute | solution.py:50
  216.5 4.1 %collective-permute-start.28 = (f32[1,96]{1,0:T(1,128)S(1)}, f32[1,96]{1,0:T(1,128)S(1)}, u32[]{:S(2)}, u32[]{:S(2)}) collective-permute-start(f32[1,96]{1,0:T(1,128)S(1)} %add.97), channel_id=1, source_target_pairs={{0,1},{1,0},{2,3},{3,2},{4,5},{5,4},{6,7},{7,6},{8,9},{9,8},{10,11... | collective-permute-start | bytes 1160 | tf_op jit(solution)/shard_map/ppermute | solution.py:138
  (134 shorter events, 56.6 us)
Async XLA Ops:
  1.7 19.7 %collective-permute-start.2 = (bf16[48,1024]{1,0:T(8,128)(2,1)S(1)}, bf16[48,1024]{1,0:T(8,128)(2,1)S(1)}, u32[]{:S(2)}, u32[]{:S(2)}) collective-permute-start(bf16[48,1024]{1,0:T(8,128)(2,1)S(1)} %get-tuple-element.39), channel_id=1, source_target_pairs={{0,32},{8,40},{16,48},{24,56},{32,64},{40,72},{48,80},{56,88},{64,... | collective-permute-start | bytes 294920 | tf_op jit(solution)/shard_map/ppermute | solution.py:58
  3.8 18.3 %collective-permute-start.3 = (bf16[48,1024]{1,0:T(8,128)(2,1)S(1)}, bf16[48,1024]{1,0:T(8,128)(2,1)S(1)}, u32[]{:S(2)}, u32[]{:S(2)}) collective-permute-start(bf16[48,1024]{1,0:T(8,128)(2,1)S(1)} %get-tuple-element.39), channel_id=1, source_target_pairs={{0,64},{8,72},{16,80},{24,88},{32,96},{40,104},{48,112},{56,120},{... | collective-permute-start | bytes 294920 | tf_op jit(solution)/shard_map/ppermute | solution.py:58
  6.3 17.7 %collective-permute-start.4 = (bf16[48,1024]{1,0:T(8,128)(2,1)S(1)}, bf16[48,1024]{1,0:T(8,128)(2,1)S(1)}, u32[]{:S(2)}, u32[]{:S(2)}) collective-permute-start(bf16[48,1024]{1,0:T(8,128)(2,1)S(1)} %get-tuple-element.39), channel_id=1, source_target_pairs={{0,96},{8,104},{16,112},{24,120},{32,0},{40,8},{48,16},{56,24},{64... | collective-permute-start | bytes 294920 | tf_op jit(solution)/shard_map/ppermute | solution.py:58
  7.4 17.3 %collective-permute-start.10 = (bf16[48,1024]{1,0:T(8,128)(2,1)S(1)}, bf16[48,1024]{1,0:T(8,128)(2,1)S(1)}, u32[]{:S(2)}, u32[]{:S(2)}) collective-permute-start(bf16[48,1024]{1,0:T(8,128)(2,1)S(1)} %get-tuple-element.40), channel_id=1, source_target_pairs={{0,192},{8,200},{16,208},{24,216},{32,224},{40,232},{48,240},{56,2... | collective-permute-start | bytes 294920 | tf_op jit(solution)/shard_map/ppermute | solution.py:59
  15.9 10.1 %collective-permute-start.11 = (bf16[48,1024]{1,0:T(8,128)(2,1)S(1)}, bf16[48,1024]{1,0:T(8,128)(2,1)S(1)}, u32[]{:S(2)}, u32[]{:S(2)}) collective-permute-start(bf16[48,1024]{1,0:T(8,128)(2,1)S(1)} %get-tuple-element.40), channel_id=1, source_target_pairs={{0,224},{8,232},{16,240},{24,248},{32,128},{40,136},{48,144},{56,1... | collective-permute-start | bytes 294920 | tf_op jit(solution)/shard_map/ppermute | solution.py:59
  17.9 12.8 %all-to-all-start = ((f32[16,2,1024]{2,1,0:T(2,128)}), f32[16,2,1024]{2,1,0:T(2,128)S(1)}, u32[]{:S(2)}, u32[]{:S(2)}) async-start(f32[16,2,1024]{2,1,0:T(2,128)} %broadcast_in_dim.8), calls=%async_computation | async-start | bytes 262144 | tf_op jit(solution)/shard_map/all_to_all | solution.py:38
  21.4 6.3 %collective-permute-start.8 = (bf16[48,1024]{1,0:T(8,128)(2,1)S(1)}, bf16[48,1024]{1,0:T(8,128)(2,1)S(1)}, u32[]{:S(2)}, u32[]{:S(2)}) collective-permute-start(bf16[48,1024]{1,0:T(8,128)(2,1)S(1)} %get-tuple-element.40), channel_id=1, source_target_pairs={{0,128},{8,136},{16,144},{24,152},{32,160},{40,168},{48,176},{56,1... | collective-permute-start | bytes 294920 | tf_op jit(solution)/shard_map/ppermute | solution.py:59
  22.1 7.2 %collective-permute-start.9 = (bf16[48,1024]{1,0:T(8,128)(2,1)S(1)}, bf16[48,1024]{1,0:T(8,128)(2,1)S(1)}, u32[]{:S(2)}, u32[]{:S(2)}) collective-permute-start(bf16[48,1024]{1,0:T(8,128)(2,1)S(1)} %get-tuple-element.40), channel_id=1, source_target_pairs={{0,160},{8,168},{16,176},{24,184},{32,192},{40,200},{48,208},{56,2... | collective-permute-start | bytes 294920 | tf_op jit(solution)/shard_map/ppermute | solution.py:59
  23.9 34.3 %collective-permute-start = (bf16[256,1024]{1,0:T(8,128)(2,1)}, bf16[256,1024]{1,0:T(8,128)(2,1)}, u32[]{:S(2)}, u32[]{:S(2)}) collective-permute-start(bf16[256,1024]{1,0:T(8,128)(2,1)} %get-tuple-element.24), channel_id=1, source_target_pairs={{0,128},{128,0},{1,129},{129,1},{2,130},{130,2},{3,131},{131,3},{4... | collective-permute-start | bytes 1572872 | tf_op jit(solution)/shard_map/ppermute | solution.py:50
  24.8 11.0 %collective-permute-start.5 = (bf16[4,48,1024]{2,1,0:T(8,128)(2,1)S(1)}, bf16[4,48,1024]{2,1,0:T(8,128)(2,1)S(1)}, u32[]{:S(2)}, u32[]{:S(2)}) collective-permute-start(bf16[4,48,1024]{2,1,0:T(8,128)(2,1)S(1)} %pad_maximum_fusion.1), channel_id=1, source_target_pairs={{0,8},{8,16},{16,24},{24,0},{32,40},{40,48},{48,56},{56,32},{64,72... | collective-permute-start | bytes 1179656 | tf_op jit(solution)/shard_map/ppermute | solution.py:68
  26.0 19.1 %collective-permute-start.6 = (bf16[4,48,1024]{2,1,0:T(8,128)(2,1)S(1)}, bf16[4,48,1024]{2,1,0:T(8,128)(2,1)S(1)}, u32[]{:S(2)}, u32[]{:S(2)}) collective-permute-start(bf16[4,48,1024]{2,1,0:T(8,128)(2,1)S(1)} %pad_maximum_fusion.1), channel_id=1, source_target_pairs={{0,16},{8,24},{16,0},{24,8},{32,48},{40,56},{48,32},{56,40},{64,80... | collective-permute-start | bytes 1179656 | tf_op jit(solution)/shard_map/ppermute | solution.py:68
  27.8 18.9 %collective-permute-start.7 = (bf16[4,48,1024]{2,1,0:T(8,128)(2,1)S(1)}, bf16[4,48,1024]{2,1,0:T(8,128)(2,1)S(1)}, u32[]{:S(2)}, u32[]{:S(2)}) collective-permute-start(bf16[4,48,1024]{2,1,0:T(8,128)(2,1)S(1)} %pad_maximum_fusion.1), channel_id=1, source_target_pairs={{0,24},{8,0},{16,8},{24,16},{32,56},{40,32},{48,40},{56,48},{64,88... | collective-permute-start | bytes 1179656 | tf_op jit(solution)/shard_map/ppermute | solution.py:68
  29.4 17.4 %collective-permute-start.12 = (bf16[4,48,1024]{2,1,0:T(8,128)(2,1)S(1)}, bf16[4,48,1024]{2,1,0:T(8,128)(2,1)S(1)}, u32[]{:S(2)}, u32[]{:S(2)}) collective-permute-start(bf16[4,48,1024]{2,1,0:T(8,128)(2,1)S(1)} %pad_maximum_fusion.2), channel_id=1, source_target_pairs={{0,32},{8,40},{16,48},{24,56},{32,64},{40,72},{48,80},{56,88},{64,... | collective-permute-start | bytes 1179656 | tf_op jit(solution)/shard_map/ppermute | solution.py:69
  35.8 12.2 %collective-permute-start.13 = (bf16[4,48,1024]{2,1,0:T(8,128)(2,1)S(1)}, bf16[4,48,1024]{2,1,0:T(8,128)(2,1)S(1)}, u32[]{:S(2)}, u32[]{:S(2)}) collective-permute-start(bf16[4,48,1024]{2,1,0:T(8,128)(2,1)S(1)} %pad_maximum_fusion.2), channel_id=1, source_target_pairs={{0,64},{8,72},{16,80},{24,88},{32,96},{40,104},{48,112},{56,120},{... | collective-permute-start | bytes 1179656 | tf_op jit(solution)/shard_map/ppermute | solution.py:69
  45.1 11.3 %collective-permute-start.14 = (bf16[4,48,1024]{2,1,0:T(8,128)(2,1)S(1)}, bf16[4,48,1024]{2,1,0:T(8,128)(2,1)S(1)}, u32[]{:S(2)}, u32[]{:S(2)}) collective-permute-start(bf16[4,48,1024]{2,1,0:T(8,128)(2,1)S(1)} %pad_maximum_fusion.2), channel_id=1, source_target_pairs={{0,96},{8,104},{16,112},{24,120},{32,0},{40,8},{48,16},{56,24},{64... | collective-permute-start | bytes 1179656 | tf_op jit(solution)/shard_map/ppermute | solution.py:69
  63.2 20.6 %all-to-all-start.1 = ((f32[16,3,512]{2,1,0:T(4,128)}), f32[16,3,512]{2,1,0:T(4,128)S(1)}, u32[]{:S(2)}, u32[]{:S(2)}) async-start(f32[16,3,512]{2,1,0:T(4,128)} %broadcast_in_dim.10), calls=%async_computation.1 | async-start | bytes 262144 | tf_op jit(solution)/shard_map/all_to_all | solution.py:38
  94.1 10.6 %collective-permute-start.16 = (f32[128,768]{1,0:T(8,128)S(1)}, f32[128,768]{1,0:T(8,128)S(1)}, u32[]{:S(2)}, u32[]{:S(2)}) collective-permute-start(f32[128,768]{1,0:T(8,128)S(1)} %get-tuple-element.25), channel_id=1, source_target_pairs={{0,128},{128,0},{1,129},{129,1},{2,130},{130,2},{3,131},{131,3},{4... | collective-permute-start | bytes 1179656 | tf_op jit(solution)/shard_map/ppermute | solution.py:50
  94.4 11.5 %collective-permute-start.17 = (f32[128,768]{1,0:T(8,128)S(1)}, f32[128,768]{1,0:T(8,128)S(1)}, u32[]{:S(2)}, u32[]{:S(2)}) collective-permute-start(f32[128,768]{1,0:T(8,128)S(1)} %get-tuple-element.26), channel_id=1, source_target_pairs={{0,134},{2,128},{4,130},{6,132},{128,2},{130,4},{132,6},{134,0},{1... | collective-permute-start | bytes 1179656 | tf_op jit(solution)/shard_map/ppermute | solution.py:51
  151.4 6.3 %collective-permute-start.20 = (bf16[256,1536]{1,0:T(8,128)(2,1)S(1)}, bf16[256,1536]{1,0:T(8,128)(2,1)S(1)}, u32[]{:S(2)}, u32[]{:S(2)}) collective-permute-start(bf16[256,1536]{1,0:T(8,128)(2,1)S(1)} %maximum_select_fusion.4), channel_id=1, source_target_pairs={{0,1},{1,0},{2,3},{3,2},{4,5},{5,4},{6,7},{7,6},{8,9},{9,8},{10,11... | collective-permute-start | bytes 2359304 | tf_op jit(solution)/shard_map/ppermute | solution.py:134
  161.2 60.7 %all-to-all-start.4 = ((bf16[32,48,1024]{2,1,0:T(8,128)(2,1)}), bf16[32,48,1024]{2,1,0:T(8,128)(2,1)S(1)}, u32[]{:S(2)}, u32[]{:S(2)}) async-start(bf16[32,48,1024]{2,1,0:T(8,128)(2,1)} %bitcast.115), calls=%async_computation.4 | async-start | bytes 6291456 | tf_op jit(solution)/shard_map/all_to_all | solution.py:142
  167.3 35.8 %collective-permute-start.21 = (f32[1,96]{1,0:T(1,128)S(1)}, f32[1,96]{1,0:T(1,128)S(1)}, u32[]{:S(2)}, u32[]{:S(2)}) collective-permute-start(f32[1,96]{1,0:T(1,128)S(1)} %fusion.9), channel_id=1, source_target_pairs={{0,32},{32,64},{64,96},{96,0},{1,33},{33,65},{65,97},{97,1},{2,34}... | collective-permute-start | bytes 1160 | tf_op jit(solution)/shard_map/ppermute | solution.py:126
  168.6 34.5 %collective-permute-start.22 = (f32[1,96]{1,0:T(1,128)S(1)}, f32[1,96]{1,0:T(1,128)S(1)}, u32[]{:S(2)}, u32[]{:S(2)}) collective-permute-start(f32[1,96]{1,0:T(1,128)S(1)} %fusion.9), channel_id=1, source_target_pairs={{0,64},{32,96},{64,0},{96,32},{1,65},{33,97},{65,1},{97,33},{2,66}... | collective-permute-start | bytes 1160 | tf_op jit(solution)/shard_map/ppermute | solution.py:126
  171.0 32.1 %collective-permute-start.23 = (f32[1,96]{1,0:T(1,128)S(1)}, f32[1,96]{1,0:T(1,128)S(1)}, u32[]{:S(2)}, u32[]{:S(2)}) collective-permute-start(f32[1,96]{1,0:T(1,128)S(1)} %fusion.9), channel_id=1, source_target_pairs={{0,96},{32,0},{64,32},{96,64},{1,97},{33,1},{65,33},{97,65},{2,98}... | collective-permute-start | bytes 1160 | tf_op jit(solution)/shard_map/ppermute | solution.py:126
  203.1 7.4 %collective-permute-start.24 = (f32[1,96]{1,0:T(1,128)S(1)}, f32[1,96]{1,0:T(1,128)S(1)}, u32[]{:S(2)}, u32[]{:S(2)}) collective-permute-start(f32[1,96]{1,0:T(1,128)S(1)} %add_add_fusion.1), channel_id=1, source_target_pairs={{0,8},{8,16},{16,24},{24,0},{1,9},{9,17},{17,25},{25,1},{2,10},{10... | collective-permute-start | bytes 1160 | tf_op jit(solution)/shard_map/ppermute | solution.py:126
  (18 other events, 83.5 us)

commit v2 on v1

--- a/solution.py
+++ b/solution.py
@@ -1,6 +1,8 @@
 import jax
 import jax.numpy as jnp
 from jax import lax
+from jax.experimental import pallas as pl
+from jax.experimental.pallas import tpu as pltpu
 from jax.sharding import Mesh, PartitionSpec as P
 
 SIDE = 128
@@ -31,6 +33,26 @@
     return [
         lax.select_n(position, *[slots[(place - p) % 4] for p in range(4)]) for place in range(4)
     ]
+
+
+def put_kernel(at, *refs):
+    out = refs[8]
+    for group in range(2):
+        block = (at[0] + group) % 2
+        for s in range(4):
+            p = (at[1 + group] + s) % 4
+            for j in range(4):
+                out[jnp.where(block == 0, j * 4 + p, 16 + p * 4 + j)] = refs[4 * group + s][j]
+
+
+def put_together(at, parts):
+    vmem = pl.BlockSpec(memory_space=pltpu.VMEM)
+    return pl.pallas_call(
+        put_kernel,
+        in_specs=[pl.BlockSpec(memory_space=pltpu.SMEM)] + [vmem] * 8,
+        out_specs=vmem,
+        out_shape=jax.ShapeDtypeStruct((32,) + parts[0].shape[1:], parts[0].dtype),
+    )(at, *parts)
 
 
 def spread(value, axes, count):
@@ -83,9 +105,9 @@
     sums = sums.reshape(2, 2, rows)
     sums = jnp.where(core == 0, sums, sums[:, ::-1])
     count = jnp.broadcast_to(jnp.sum(weight), (1, 2, rows))
-    totals = spread(
-        jnp.concatenate([sums, count]).reshape(3, 2 * rows), ("zl", "zh", "c"), 16
-    )
+    sums = jnp.concatenate([sums, count]).reshape(3, 2 * rows)
+    sums = sums + lax.ppermute(sums, "c", PAIR)
+    totals = spread(sums, ("zl", "zh"), 8)
     totals = jnp.sum(totals, 0)
     totals = totals.reshape(3, 2, rows)
     totals = jnp.where(core == 0, totals, totals[:, ::-1]).reshape(3, 2 * rows)
@@ -93,11 +115,8 @@
     bg_std = jnp.sqrt(totals[1] / totals[2] - bg_mean * bg_mean + EPSILON)
     normed = ((whitened - bg_mean[:, None]) / bg_std[:, None]).astype(BF16)
 
-    same2, cross2 = ring_order(same2, side), ring_order(cross2, near)
-    a = jnp.where(zl == 0, jnp.stack(same2, 1), jnp.stack(cross2, 1))
-    b = jnp.where(zl == 0, jnp.stack(cross2), jnp.stack(same2))
-    refs = jnp.stack([a, b]).reshape(32 * views, half)
-
+    refs = put_together(jnp.stack([zl, side, near]), same2 + cross2)
+    refs = refs.reshape(32 * views, half)
     ref_energy = jnp.sum(jnp.square(refs.astype(F32)), 1)
     score = lambda a: (
         lax.dot_general(a, refs, (((1,), (1,)), ((), ())), preferred_element_type=F32)
@@ -122,10 +141,8 @@
     class_mass = jnp.sum(strip, 0, dtype=F32)
     onehot = (view_class[:, None] == jnp.arange(NCLS, dtype=jnp.int32)[None, :]).astype(F32)
     share = jnp.dot(class_mass[None], onehot, precision=lax.Precision.HIGHEST)
-    around = lambda a, axis: a + sum(
-        lax.ppermute(a, axis, [(i, (i + s) % 4) for i in range(4)]) for s in (1, 2, 3)
-    )
-    share = around(share, "x")
+    share = spread(share, ("x", "y"), 16)
+    share = jnp.sum(share, 0)
     other_strip = [swap(strip[:, :cut]), far(strip[:, cut:])]
     other_strip = jnp.concatenate(other_strip, 1)
     gathered = jnp.where(
@@ -133,7 +150,6 @@
     )
     gathered_c = lax.ppermute(gathered, "c", PAIR)
     gathered = jnp.concatenate([gathered, gathered_c])
-    share = around(share, "y")
     share = share + swap(share)
     share = share + lax.ppermute(share, "c", PAIR)
 

time: 224 us -> 212 us (0.946)
  the two profiles are of different devices: /device:TPU:1 before, /device:TPU:56 now
where the time goes in v2:
time: 212 us; the launch traced here: 211 us
  waiting for transfers between devices  80.9 us (38%)
  starting transfers between devices  55.5 us (26%)
  blocking collectives  39.5 us (19%)
  other arithmetic  16.8 us (8%)
  matrix products  8.2 us (4%)
  local copies, waits for them, and re-layouts  5.65 us (3%)
  Pallas kernels  3.71 us (2%)
    ppermute x5, waiting for transfers between devices, on_device(): swap = lambda a: lax.ppermute(a, 'zl', PAIR)  52.3 us
    all_to_all x3, starting transfers between devices, spread(): return lax.all_to_all(sent, axes, split_axis=0, concat_axis=0)  22.1 us
    all_to_all x1, blocking collectives, on_device(): lax.all_to_all(kept.reshape(4, 32, -1), 'zh', split_axis=0, concat_axis=0)  21.6 us
    all_to_all x1, blocking collectives, spread(): return lax.all_to_all(sent, axes, split_axis=0, concat_axis=0)  17.9 us
    ppermute x5, starting transfers between devices, on_device(): swap = lambda a: lax.ppermute(a, 'zl', PAIR)  8.58 us
    all_to_all x3, waiting for transfers between devices, spread(): return lax.all_to_all(sent, axes, split_axis=0, concat_axis=0)  7.98 us
    all_to_all x1, starting transfers between devices, on_device(): part = lax.all_to_all(part, img, split_axis=0, concat_axis=0)  6.64 us
    ppermute x3, waiting for transfers between devices, on_device(): lax.ppermute(cross, img, plane(1, s, False))  5.29 us
  transfers between devices with their start and end apart: 28, of which 18 were waited for; matrix products, arithmetic and copies ran while one was open for 8% of the time, Pallas kernels for 2%

profile of v2, /device:TPU:56, one launch (start us, length us, event | category | flops | bytes accessed | tf_op | source)
XLA Modules:
  0.0 211.3 jit_solution(14483773321815303654)
XLA Ops:
  2.1 4.6 %collective-permute-start.11 = (bf16[48,1024]{1,0:T(8,128)(2,1)S(1)}, bf16[48,1024]{1,0:T(8,128)(2,1)}, u32[]{:S(2)}, u32[]{:S(2)}) collective-permute-start(bf16[48,1024]{1,0:T(8,128)(2,1)S(1)} %get-tuple-element.33), channel_id=1, source_target_pairs={{0,192},{8,200},{16,208},{24,216},{32,224},{40,232},{48,240},{56,2... | collective-permute-start | bytes 294920 | tf_op jit(solution)/shard_map/ppermute | solution.py:81
  6.7 3.6 %collective-permute-start.4 = (bf16[48,1024]{1,0:T(8,128)(2,1)S(1)}, bf16[48,1024]{1,0:T(8,128)(2,1)S(1)}, u32[]{:S(2)}, u32[]{:S(2)}) collective-permute-start(bf16[48,1024]{1,0:T(8,128)(2,1)S(1)} %get-tuple-element.34), channel_id=1, source_target_pairs={{0,64},{8,72},{16,80},{24,88},{32,96},{40,104},{48,112},{56,120},{... | collective-permute-start | bytes 294920 | tf_op jit(solution)/shard_map/ppermute | solution.py:80
  16.5 2.6 %collective-permute-done.1 = f32[2,1024]{1,0:T(2,128)S(1)} collective-permute-done((f32[2,1024]{1,0:T(2,128)S(1)}, f32[2,1024]{1,0:T(2,128)S(1)}, u32[]{:S(2)}, u32[]{:S(2)}) %collective-permute-start.1) | collective-permute-done | bytes 8224 | tf_op jit(solution)/shard_map/ppermute | solution.py:72
  20.4 7.8 %all-to-all-start = ((f32[16,2,1024]{2,1,0:T(2,128)}), f32[16,2,1024]{2,1,0:T(2,128)S(1)}, u32[]{:S(2)}, u32[]{:S(2)}) async-start(f32[16,2,1024]{2,1,0:T(2,128)} %broadcast_in_dim.8), calls=%async_computation | async-start | bytes 262144 | tf_op jit(solution)/shard_map/all_to_all | solution.py:60
  28.3 3.1 %collective-permute-start.7 = (bf16[4,48,1024]{2,1,0:T(8,128)(2,1)S(1)}, bf16[4,48,1024]{2,1,0:T(8,128)(2,1)S(1)}, u32[]{:S(2)}, u32[]{:S(2)}) collective-permute-start(bf16[4,48,1024]{2,1,0:T(8,128)(2,1)S(1)} %pad_maximum_fusion.refs_0_), channel_id=1, source_target_pairs={{0,16},{8,24},{16,0},{24,8},{32,48},{40,56},{48,32},{56,40},{64,80... | collective-permute-start | bytes 1179656 | tf_op jit(solution)/shard_map/ppermute | solution.py:90
  34.9 2.4 %collective-permute-start.14 = (bf16[4,48,1024]{2,1,0:T(8,128)(2,1)S(1)}, bf16[4,48,1024]{2,1,0:T(8,128)(2,1)}, u32[]{:S(2)}, u32[]{:S(2)}) collective-permute-start(bf16[4,48,1024]{2,1,0:T(8,128)(2,1)S(1)} %pad_maximum_fusion.1.refs_4_), channel_id=1, source_target_pairs={{0,64},{8,72},{16,80},{24,88},{32,96},{40,104},{48,112},{56,120},{... | collective-permute-start | bytes 1179656 | tf_op jit(solution)/shard_map/ppermute | solution.py:91
  39.7 3.2 %collective-permute-start = (bf16[256,1024]{1,0:T(8,128)(2,1)S(1)}, bf16[256,1024]{1,0:T(8,128)(2,1)S(1)}, u32[]{:S(2)}, u32[]{:S(2)}) collective-permute-start(bf16[256,1024]{1,0:T(8,128)(2,1)S(1)} %get-tuple-element.18), channel_id=1, source_target_pairs={{0,128},{128,0},{1,129},{129,1},{2,130},{130,2},{3,131},{131,3},{4... | collective-permute-start | bytes 1572872 | tf_op jit(solution)/shard_map/ppermute | solution.py:72
  43.0 3.7 %collective-permute-done.6.refs_1_ = bf16[4,48,1024]{2,1,0:T(8,128)(2,1)S(1)} collective-permute-done((bf16[4,48,1024]{2,1,0:T(8,128)(2,1)S(1)}, bf16[4,48,1024]{2,1,0:T(8,128)(2,1)S(1)}, u32[]{:S(2)}, u32[]{:S(2)}) %collective-permute-start.6) | collective-permute-done | bytes 393248 | tf_op jit(solution)/shard_map/ppermute | solution.py:90
  47.8 4.3 %collective-permute-done.13.refs_5_ = bf16[4,48,1024]{2,1,0:T(8,128)(2,1)} collective-permute-done((bf16[4,48,1024]{2,1,0:T(8,128)(2,1)S(1)}, bf16[4,48,1024]{2,1,0:T(8,128)(2,1)}, u32[]{:S(2)}, u32[]{:S(2)}) %collective-permute-start.13) | collective-permute-done | bytes 393248 | tf_op jit(solution)/shard_map/ppermute | solution.py:91
  52.1 3.7 %shard_map.67 = bf16[32,48,1024]{2,1,0:T(8,128)(2,1)} custom-call(s32[3]{0:T(128)} %pad_add_fusion.at, bf16[4,48,1024]{2,1,0:T(8,128)(2,1)} %copy-done.2, bf16[4,48,1024]{2,1,0:T(8,128)(2,1)} %copy-done.8, bf16[4,48,1024]{2,1,0:T(8,128)(2,1)} %copy-done.7, bf16[4,48,1024]{2,1,0:T(8,128)(2,1)} %copy-done.6, bf16[4,48,1024]{2,1,0:T(8,128)(2,1)} %copy-done.3, ...), custom_call_target="tpu_custom_call" | custom-call | tf_op jit(solution)/shard_map/pallas_call | solution.py:50
  55.8 2.6 %multiply_reduce_fusion = f32[32,48]{1,0:T(8,128)S(1)} fusion(bf16[32,48,1024]{2,1,0:T(8,128)(2,1)} %shard_map.67), kind=kLoop, calls=%fused_computation.1 | loop fusion | flops 4717056 | bytes 3151872 | tf_op jit(solution)/shard_map/reduce_sum | solution.py:120
  62.7 8.1 %all-to-all-start.1 = ((f32[8,3,512]{2,1,0:T(4,128)}), f32[8,3,512]{2,1,0:T(4,128)S(1)}, u32[]{:S(2)}, u32[]{:S(2)}) async-start(f32[8,3,512]{2,1,0:T(4,128)} %broadcast_in_dim.9), calls=%async_computation.1 | async-start | bytes 131072 | tf_op jit(solution)/shard_map/all_to_all | solution.py:60
  72.4 5.4 %all-to-all-done.1 = f32[8,3,512]{2,1,0:T(4,128)S(1)} async-done(((f32[8,3,512]{2,1,0:T(4,128)}), f32[8,3,512]{2,1,0:T(4,128)S(1)}, u32[]{:S(2)}, u32[]{:S(2)}) %all-to-all-start.1) | async-done | bytes 49184 | tf_op jit(solution)/shard_map/all_to_all | solution.py:60
  79.9 2.2 %convolution_subtract_fusion.1 = f32[256,1536]{1,0:T(8,128)} fusion(bf16[1536,1024]{1,0:T(8,128)(2,1)S(1)} %bitcast.77, f32[1536]{0:T(1024)S(1)} %mul.86, bf16[512,1024]{1,0:T(8,128)(2,1)S(1)} %fusion.4), kind=kOutput, calls=%fused_computation.4 | convolution fusion | flops 805699584 | bytes 5251072 | tf_op jit(solution)/shard_map/dot_general | solution.py:122
  88.8 10.1 %collective-permute-done.17 = f32[128,768]{1,0:T(8,128)S(1)} collective-permute-done((f32[128,768]{1,0:T(8,128)S(1)}, f32[128,768]{1,0:T(8,128)S(1)}, u32[]{:S(2)}, u32[]{:S(2)}) %collective-permute-start.17) | collective-permute-done | bytes 393248 | tf_op jit(solution)/shard_map/ppermute | solution.py:72
  99.6 21.6 %all_to_all.30 = f32[4,32,1536]{2,1,0:T(8,128)S(1)} all-to-all(f32[4,32,1536]{2,1,0:T(8,128)S(1)} %maximum_add_fusion), channel_id=1, replica_groups=mesh['zl'=2,'x'=4,'y'=4,'zh'=4,'c'=2] {'zh'}, dimensions={0} | all-to-all | bytes 1572864 | tf_op jit(solution)/shard_map/all_to_all | solution.py:132
  122.2 17.9 %all_to_all.31 = bf16[4,32,1536]{2,1,0:T(8,128)(2,1)S(1)} all-to-all(bf16[4,32,1536]{2,1,0:T(8,128)(2,1)S(1)} %broadcast_in_dim.10), channel_id=1, replica_groups=mesh['zl'=2,'x'=4,'y'=4,'zh'=4,'c'=2] {'zh'}, dimensions={0} | all-to-all | bytes 786432 | tf_op jit(solution)/shard_map/all_to_all | solution.py:60
  140.2 2.4 %collective-permute-start.19 = (bf16[128,768]{1,0:T(8,128)(2,1)S(1)}, bf16[128,768]{1,0:T(8,128)(2,1)S(1)}, u32[]{:S(2)}, u32[]{:S(2)}) collective-permute-start(bf16[128,768]{1,0:T(8,128)(2,1)S(1)} %get-tuple-element.24), channel_id=1, source_target_pairs={{0,128},{128,0},{1,129},{129,1},{2,130},{130,2},{3,131},{131,3},{4... | collective-permute-start | bytes 589832 | tf_op jit(solution)/shard_map/ppermute | solution.py:72
  142.6 3.6 %collective-permute-done.19 = bf16[128,768]{1,0:T(8,128)(2,1)S(1)} collective-permute-done((bf16[128,768]{1,0:T(8,128)(2,1)S(1)}, bf16[128,768]{1,0:T(8,128)(2,1)S(1)}, u32[]{:S(2)}, u32[]{:S(2)}) %collective-permute-start.19) | collective-permute-done | bytes 196640 | tf_op jit(solution)/shard_map/ppermute | solution.py:72
  149.7 6.1 %all-to-all-start.5 = ((f32[16,1,96]{2,1,0:T(1,128)}), f32[16,1,96]{2,1,0:T(1,128)S(1)}, u32[]{:S(2)}, u32[]{:S(2)}) async-start(f32[16,1,96]{2,1,0:T(1,128)} %broadcast_in_dim.11), calls=%async_computation.5 | async-start | bytes 16384 | tf_op jit(solution)/shard_map/all_to_all | solution.py:60
  155.8 3.5 %convolution_convert_fusion = bf16[1536,1024]{1,0:T(8,128)(2,1)} fusion(bf16[512,1024]{1,0:T(8,128)(2,1)S(1)} %copy-done.5, bf16[256,1536]{1,0:T(8,128)(2,1)S(1)} %collective-permute-done.21, bf16[256,1536]{1,0:T(8,128)(2,1)S(1)} %maximum_select_fusion.2), kind=kOutput, calls=%fused_computation.2 | convolution fusion | flops 1615331328 | bytes 5767168 | tf_op jit(solution)/shard_map/dot_general | solution.py:156
  161.4 6.6 %all-to-all-start.4 = ((bf16[32,48,1024]{2,1,0:T(8,128)(2,1)}), bf16[32,48,1024]{2,1,0:T(8,128)(2,1)S(1)}, u32[]{:S(2)}, u32[]{:S(2)}) async-start(bf16[32,48,1024]{2,1,0:T(8,128)(2,1)} %bitcast.82), calls=%async_computation.4 | async-start | bytes 6291456 | tf_op jit(solution)/shard_map/all_to_all | solution.py:158
  168.6 35.9 %collective-permute-done.22 = f32[1,96]{1,0:T(1,128)S(1)} collective-permute-done((f32[1,96]{1,0:T(1,128)S(1)}, f32[1,96]{1,0:T(1,128)S(1)}, u32[]{:S(2)}, u32[]{:S(2)}) %collective-permute-start.22) | collective-permute-done | bytes 416 | tf_op jit(solution)/shard_map/ppermute | solution.py:72
  206.2 3.7 %all-to-all-done.4 = bf16[32,48,1024]{2,1,0:T(8,128)(2,1)S(1)} async-done(((bf16[32,48,1024]{2,1,0:T(8,128)(2,1)}), bf16[32,48,1024]{2,1,0:T(8,128)(2,1)S(1)}, u32[]{:S(2)}, u32[]{:S(2)}) %all-to-all-start.4) | async-done | bytes 3145760 | tf_op jit(solution)/shard_map/all_to_all | solution.py:158
  (128 shorter events, 41.5 us)
Async XLA Ops:
  1.7 26.6 %collective-permute-start.12 = (bf16[48,1024]{1,0:T(8,128)(2,1)S(1)}, bf16[48,1024]{1,0:T(8,128)(2,1)}, u32[]{:S(2)}, u32[]{:S(2)}) collective-permute-start(bf16[48,1024]{1,0:T(8,128)(2,1)S(1)} %get-tuple-element.33), channel_id=1, source_target_pairs={{0,224},{8,232},{16,240},{24,248},{32,128},{40,136},{48,144},{56,1... | collective-permute-start | bytes 294920 | tf_op jit(solution)/shard_map/ppermute | solution.py:81
  2.1 29.3 %collective-permute-start.11 = (bf16[48,1024]{1,0:T(8,128)(2,1)S(1)}, bf16[48,1024]{1,0:T(8,128)(2,1)}, u32[]{:S(2)}, u32[]{:S(2)}) collective-permute-start(bf16[48,1024]{1,0:T(8,128)(2,1)S(1)} %get-tuple-element.33), channel_id=1, source_target_pairs={{0,192},{8,200},{16,208},{24,216},{32,224},{40,232},{48,240},{56,2... | collective-permute-start | bytes 294920 | tf_op jit(solution)/shard_map/ppermute | solution.py:81
  6.7 6.7 %collective-permute-start.5 = (bf16[48,1024]{1,0:T(8,128)(2,1)S(1)}, bf16[48,1024]{1,0:T(8,128)(2,1)S(1)}, u32[]{:S(2)}, u32[]{:S(2)}) collective-permute-start(bf16[48,1024]{1,0:T(8,128)(2,1)S(1)} %get-tuple-element.34), channel_id=1, source_target_pairs={{0,96},{8,104},{16,112},{24,120},{32,0},{40,8},{48,16},{56,24},{64... | collective-permute-start | bytes 294920 | tf_op jit(solution)/shard_map/ppermute | solution.py:80
  6.7 7.7 %collective-permute-start.4 = (bf16[48,1024]{1,0:T(8,128)(2,1)S(1)}, bf16[48,1024]{1,0:T(8,128)(2,1)S(1)}, u32[]{:S(2)}, u32[]{:S(2)}) collective-permute-start(bf16[48,1024]{1,0:T(8,128)(2,1)S(1)} %get-tuple-element.34), channel_id=1, source_target_pairs={{0,64},{8,72},{16,80},{24,88},{32,96},{40,104},{48,112},{56,120},{... | collective-permute-start | bytes 294920 | tf_op jit(solution)/shard_map/ppermute | solution.py:80
  10.3 4.6 %collective-permute-start.3 = (bf16[48,1024]{1,0:T(8,128)(2,1)S(1)}, bf16[48,1024]{1,0:T(8,128)(2,1)S(1)}, u32[]{:S(2)}, u32[]{:S(2)}) collective-permute-start(bf16[48,1024]{1,0:T(8,128)(2,1)S(1)} %get-tuple-element.34), channel_id=1, source_target_pairs={{0,32},{8,40},{16,48},{24,56},{32,64},{40,72},{48,80},{56,88},{64,... | collective-permute-start | bytes 294920 | tf_op jit(solution)/shard_map/ppermute | solution.py:80
  13.3 19.1 %collective-permute-start.10 = (bf16[48,1024]{1,0:T(8,128)(2,1)S(1)}, bf16[48,1024]{1,0:T(8,128)(2,1)S(1)}, u32[]{:S(2)}, u32[]{:S(2)}) collective-permute-start(bf16[48,1024]{1,0:T(8,128)(2,1)S(1)} %get-tuple-element.33), channel_id=1, source_target_pairs={{0,160},{8,168},{16,176},{24,184},{32,192},{40,200},{48,208},{56,2... | collective-permute-start | bytes 294920 | tf_op jit(solution)/shard_map/ppermute | solution.py:81
  14.4 18.8 %collective-permute-start.9 = (bf16[48,1024]{1,0:T(8,128)(2,1)S(1)}, bf16[48,1024]{1,0:T(8,128)(2,1)}, u32[]{:S(2)}, u32[]{:S(2)}) collective-permute-start(bf16[48,1024]{1,0:T(8,128)(2,1)S(1)} %get-tuple-element.33), channel_id=1, source_target_pairs={{0,128},{8,136},{16,144},{24,152},{32,160},{40,168},{48,176},{56,1... | collective-permute-start | bytes 294920 | tf_op jit(solution)/shard_map/ppermute | solution.py:81
  19.1 18.2 %collective-permute-start.8 = (bf16[4,48,1024]{2,1,0:T(8,128)(2,1)S(1)}, bf16[4,48,1024]{2,1,0:T(8,128)(2,1)S(1)}, u32[]{:S(2)}, u32[]{:S(2)}) collective-permute-start(bf16[4,48,1024]{2,1,0:T(8,128)(2,1)S(1)} %pad_maximum_fusion.refs_0_), channel_id=1, source_target_pairs={{0,8},{8,16},{16,24},{24,0},{32,40},{40,48},{48,56},{56,32},{64,72... | collective-permute-start | bytes 1179656 | tf_op jit(solution)/shard_map/ppermute | solution.py:90
  20.4 19.2 %all-to-all-start = ((f32[16,2,1024]{2,1,0:T(2,128)}), f32[16,2,1024]{2,1,0:T(2,128)S(1)}, u32[]{:S(2)}, u32[]{:S(2)}) async-start(f32[16,2,1024]{2,1,0:T(2,128)} %broadcast_in_dim.8), calls=%async_computation | async-start | bytes 262144 | tf_op jit(solution)/shard_map/all_to_all | solution.py:60
  28.3 11.5 %collective-permute-start.7 = (bf16[4,48,1024]{2,1,0:T(8,128)(2,1)S(1)}, bf16[4,48,1024]{2,1,0:T(8,128)(2,1)S(1)}, u32[]{:S(2)}, u32[]{:S(2)}) collective-permute-start(bf16[4,48,1024]{2,1,0:T(8,128)(2,1)S(1)} %pad_maximum_fusion.refs_0_), channel_id=1, source_target_pairs={{0,16},{8,24},{16,0},{24,8},{32,48},{40,56},{48,32},{56,40},{64,80... | collective-permute-start | bytes 1179656 | tf_op jit(solution)/shard_map/ppermute | solution.py:90
  31.3 15.4 %collective-permute-start.6 = (bf16[4,48,1024]{2,1,0:T(8,128)(2,1)S(1)}, bf16[4,48,1024]{2,1,0:T(8,128)(2,1)S(1)}, u32[]{:S(2)}, u32[]{:S(2)}) collective-permute-start(bf16[4,48,1024]{2,1,0:T(8,128)(2,1)S(1)} %pad_maximum_fusion.refs_0_), channel_id=1, source_target_pairs={{0,24},{8,0},{16,8},{24,16},{32,56},{40,32},{48,40},{56,48},{64,88... | collective-permute-start | bytes 1179656 | tf_op jit(solution)/shard_map/ppermute | solution.py:90
  34.3 12.5 %collective-permute-start.15 = (bf16[4,48,1024]{2,1,0:T(8,128)(2,1)S(1)}, bf16[4,48,1024]{2,1,0:T(8,128)(2,1)}, u32[]{:S(2)}, u32[]{:S(2)}) collective-permute-start(bf16[4,48,1024]{2,1,0:T(8,128)(2,1)S(1)} %pad_maximum_fusion.1.refs_4_), channel_id=1, source_target_pairs={{0,32},{8,40},{16,48},{24,56},{32,64},{40,72},{48,80},{56,88},{64,... | collective-permute-start | bytes 1179656 | tf_op jit(solution)/shard_map/ppermute | solution.py:91
  34.9 12.9 %collective-permute-start.14 = (bf16[4,48,1024]{2,1,0:T(8,128)(2,1)S(1)}, bf16[4,48,1024]{2,1,0:T(8,128)(2,1)}, u32[]{:S(2)}, u32[]{:S(2)}) collective-permute-start(bf16[4,48,1024]{2,1,0:T(8,128)(2,1)S(1)} %pad_maximum_fusion.1.refs_4_), channel_id=1, source_target_pairs={{0,64},{8,72},{16,80},{24,88},{32,96},{40,104},{48,112},{56,120},{... | collective-permute-start | bytes 1179656 | tf_op jit(solution)/shard_map/ppermute | solution.py:91
  37.3 14.7 %collective-permute-start.13 = (bf16[4,48,1024]{2,1,0:T(8,128)(2,1)S(1)}, bf16[4,48,1024]{2,1,0:T(8,128)(2,1)}, u32[]{:S(2)}, u32[]{:S(2)}) collective-permute-start(bf16[4,48,1024]{2,1,0:T(8,128)(2,1)S(1)} %pad_maximum_fusion.1.refs_4_), channel_id=1, source_target_pairs={{0,96},{8,104},{16,112},{24,120},{32,0},{40,8},{48,16},{56,24},{64... | collective-permute-start | bytes 1179656 | tf_op jit(solution)/shard_map/ppermute | solution.py:91
  39.7 18.6 %collective-permute-start = (bf16[256,1024]{1,0:T(8,128)(2,1)S(1)}, bf16[256,1024]{1,0:T(8,128)(2,1)S(1)}, u32[]{:S(2)}, u32[]{:S(2)}) collective-permute-start(bf16[256,1024]{1,0:T(8,128)(2,1)S(1)} %get-tuple-element.18), channel_id=1, source_target_pairs={{0,128},{128,0},{1,129},{129,1},{2,130},{130,2},{3,131},{131,3},{4... | collective-permute-start | bytes 1572872 | tf_op jit(solution)/shard_map/ppermute | solution.py:72
  62.7 15.0 %all-to-all-start.1 = ((f32[8,3,512]{2,1,0:T(4,128)}), f32[8,3,512]{2,1,0:T(4,128)S(1)}, u32[]{:S(2)}, u32[]{:S(2)}) async-start(f32[8,3,512]{2,1,0:T(4,128)} %broadcast_in_dim.9), calls=%async_computation.1 | async-start | bytes 131072 | tf_op jit(solution)/shard_map/all_to_all | solution.py:60
  87.7 11.2 %collective-permute-start.17 = (f32[128,768]{1,0:T(8,128)S(1)}, f32[128,768]{1,0:T(8,128)S(1)}, u32[]{:S(2)}, u32[]{:S(2)}) collective-permute-start(f32[128,768]{1,0:T(8,128)S(1)} %get-tuple-element.19), channel_id=1, source_target_pairs={{0,128},{128,0},{1,129},{129,1},{2,130},{130,2},{3,131},{131,3},{4... | collective-permute-start | bytes 1179656 | tf_op jit(solution)/shard_map/ppermute | solution.py:72
  88.6 10.9 %collective-permute-start.18 = (f32[128,768]{1,0:T(8,128)S(1)}, f32[128,768]{1,0:T(8,128)S(1)}, u32[]{:S(2)}, u32[]{:S(2)}) collective-permute-start(f32[128,768]{1,0:T(8,128)S(1)} %get-tuple-element.20), channel_id=1, source_target_pairs={{0,134},{2,128},{4,130},{6,132},{128,2},{130,4},{132,6},{134,0},{1... | collective-permute-start | bytes 1179656 | tf_op jit(solution)/shard_map/ppermute | solution.py:73
  140.2 6.0 %collective-permute-start.19 = (bf16[128,768]{1,0:T(8,128)(2,1)S(1)}, bf16[128,768]{1,0:T(8,128)(2,1)S(1)}, u32[]{:S(2)}, u32[]{:S(2)}) collective-permute-start(bf16[128,768]{1,0:T(8,128)(2,1)S(1)} %get-tuple-element.24), channel_id=1, source_target_pairs={{0,128},{128,0},{1,129},{129,1},{2,130},{130,2},{3,131},{131,3},{4... | collective-permute-start | bytes 589832 | tf_op jit(solution)/shard_map/ppermute | solution.py:72
  142.6 5.7 %collective-permute-start.20 = (bf16[128,768]{1,0:T(8,128)(2,1)S(1)}, bf16[128,768]{1,0:T(8,128)(2,1)S(1)}, u32[]{:S(2)}, u32[]{:S(2)}) collective-permute-start(bf16[128,768]{1,0:T(8,128)(2,1)S(1)} %get-tuple-element.23), channel_id=1, source_target_pairs={{0,134},{2,128},{4,130},{6,132},{128,2},{130,4},{132,6},{134,0},{1... | collective-permute-start | bytes 589832 | tf_op jit(solution)/shard_map/ppermute | solution.py:73
  148.4 7.4 %collective-permute-start.21 = (bf16[256,1536]{1,0:T(8,128)(2,1)S(1)}, bf16[256,1536]{1,0:T(8,128)(2,1)S(1)}, u32[]{:S(2)}, u32[]{:S(2)}) collective-permute-start(bf16[256,1536]{1,0:T(8,128)(2,1)S(1)} %maximum_select_fusion.2), channel_id=1, source_target_pairs={{0,1},{1,0},{2,3},{3,2},{4,5},{5,4},{6,7},{7,6},{8,9},{9,8},{10,11... | collective-permute-start | bytes 2359304 | tf_op jit(solution)/shard_map/ppermute | solution.py:151
  149.7 11.7 %all-to-all-start.5 = ((f32[16,1,96]{2,1,0:T(1,128)}), f32[16,1,96]{2,1,0:T(1,128)S(1)}, u32[]{:S(2)}, u32[]{:S(2)}) async-start(f32[16,1,96]{2,1,0:T(1,128)} %broadcast_in_dim.11), calls=%async_computation.5 | async-start | bytes 16384 | tf_op jit(solution)/shard_map/all_to_all | solution.py:60
  161.4 48.5 %all-to-all-start.4 = ((bf16[32,48,1024]{2,1,0:T(8,128)(2,1)}), bf16[32,48,1024]{2,1,0:T(8,128)(2,1)S(1)}, u32[]{:S(2)}, u32[]{:S(2)}) async-start(bf16[32,48,1024]{2,1,0:T(8,128)(2,1)} %bitcast.82), calls=%async_computation.4 | async-start | bytes 6291456 | tf_op jit(solution)/shard_map/all_to_all | solution.py:158
  168.1 36.5 %collective-permute-start.22 = (f32[1,96]{1,0:T(1,128)S(1)}, f32[1,96]{1,0:T(1,128)S(1)}, u32[]{:S(2)}, u32[]{:S(2)}) collective-permute-start(f32[1,96]{1,0:T(1,128)S(1)} %bitcast.102), channel_id=1, source_target_pairs={{0,128},{128,0},{1,129},{129,1},{2,130},{130,2},{3,131},{131,3},{4... | collective-permute-start | bytes 1160 | tf_op jit(solution)/shard_map/ppermute | solution.py:72
  (17 other events, 186.4 us)

commit v3 on v2

--- a/solution.py
+++ b/solution.py
@@ -13,45 +13,38 @@
 FAR = [(zh, 4 + (zh - 1) % 4) for zh in range(4)] + [(4 + zh, (zh + 1) % 4) for zh in range(4)]
 
 
-def place(zl, x, y):
-    return zl * 16 + x * 4 + y
-
-
-def plane(cross, step, first):
+def plane(step, first):
     pairs = []
-    for zl in range(2):
-        for x in range(4):
-            for y in range(4):
-                block = zl if first else zl ^ cross
-                along_x = (block == 0) == first
+    for x in range(4):
+        for y in range(4):
+            for core in range(2):
+                along_x = (core == 0) == first
                 to = ((x - step) % 4, y) if along_x else (x, (y - step) % 4)
-                pairs.append((place(zl, x, y), place(zl ^ cross if first else zl, *to)))
+                pairs.append((x * 8 + y * 2 + core, to[0] * 8 + to[1] * 2 + core))
     return pairs
 
 
-def ring_order(slots, position):
-    return [
-        lax.select_n(position, *[slots[(place - p) % 4] for p in range(4)]) for place in range(4)
-    ]
-
-
 def put_kernel(at, *refs):
-    out = refs[8]
-    for group in range(2):
-        block = (at[0] + group) % 2
+    out = refs[4]
+    zl, core, first, second = at[0], at[1], at[2], at[3]
+    rows = out.shape[1]
+    for t in range(4):
+        q = (second + t) % 4
         for s in range(4):
-            p = (at[1 + group] + s) % 4
-            for j in range(4):
-                out[jnp.where(block == 0, j * 4 + p, 16 + p * 4 + j)] = refs[4 * group + s][j]
+            p = (first + s) % 4
+            spot = jnp.where(core == 0, p * 4 + q, q * 4 + p)
+            for k in range(2):
+                out[(zl + k) % 2 * 16 + spot] = refs[t][s, k * rows : (k + 1) * rows]
 
 
 def put_together(at, parts):
     vmem = pl.BlockSpec(memory_space=pltpu.VMEM)
+    shape = (32, parts[0].shape[1] // 2, parts[0].shape[2])
     return pl.pallas_call(
         put_kernel,
-        in_specs=[pl.BlockSpec(memory_space=pltpu.SMEM)] + [vmem] * 8,
+        in_specs=[pl.BlockSpec(memory_space=pltpu.SMEM)] + [vmem] * 4,
         out_specs=vmem,
-        out_shape=jax.ShapeDtypeStruct((32,) + parts[0].shape[1:], parts[0].dtype),
+        out_shape=jax.ShapeDtypeStruct(shape, parts[0].dtype),
     )(at, *parts)
 
 
@@ -76,19 +69,17 @@
     local = jnp.stack([jnp.sum(widened, 0), jnp.sum(widened * widened, 0)])
     moments = swap(theirs(local, 1))
     moments = mine(local, 1) + moments
-    ref_own, ref_other = mine(references, 1), theirs(references, 1)
-    same = [ref_own] + [lax.ppermute(ref_own, img, plane(0, s, True)) for s in (1, 2, 3)]
-    cross = [lax.ppermute(ref_other, img, plane(1, s, True)) for s in (0, 1, 2, 3)]
+    plan = ("x", "y", "c")
+    ref_other = swap(theirs(references, 1))
+    ref_pair = jnp.concatenate([mine(references, 1), ref_other])
+    line = [lax.ppermute(ref_pair, plan, plane(s, True)) for s in (1, 2, 3)]
     img_other = swap(theirs(images, 1))
     img_own = mine(images, 1)
-    moments = jnp.sum(spread(moments, ("x", "y"), 16), 0)
+    moments = spread(moments, ("x", "y"), 16)
+    moments = jnp.sum(moments, 0)
 
-    near = jnp.where(zl == 0, x, y)
-    side = jnp.where(zl == 0, y, x)
-    same = jnp.stack(ring_order(same, near))
-    cross = jnp.stack(ring_order(cross, side))
-    same2 = [same] + [lax.ppermute(same, img, plane(0, s, False)) for s in (1, 2, 3)]
-    cross2 = [cross] + [lax.ppermute(cross, img, plane(1, s, False)) for s in (1, 2, 3)]
+    line = jnp.stack([ref_pair] + line)
+    sheet = [line] + [lax.ppermute(line, plan, plane(s, False)) for s in (1, 2, 3)]
 
     shape = (4, 2, 32, half)
     own, other = img_own.reshape(shape), img_other.reshape(shape)
@@ -115,7 +106,8 @@
     bg_std = jnp.sqrt(totals[1] / totals[2] - bg_mean * bg_mean + EPSILON)
     normed = ((whitened - bg_mean[:, None]) / bg_std[:, None]).astype(BF16)
 
-    refs = put_together(jnp.stack([zl, side, near]), same2 + cross2)
+    first, second = jnp.where(core == 0, x, y), jnp.where(core == 0, y, x)
+    refs = put_together(jnp.stack([zl, core, first, second]), sheet)
     refs = refs.reshape(32 * views, half)
     ref_energy = jnp.sum(jnp.square(refs.astype(F32)), 1)
     score = lambda a: (

time: 212 us -> 195 us (0.920)
  waiting for transfers between devices: 80.9 us -> 71.4 us
  starting transfers between devices: 55.5 us -> 46.3 us
  blocking collectives: 39.5 us -> 43.4 us
  other arithmetic: 16.8 us -> 14.3 us
    ppermute x13 -> x6, starting transfers between devices: 17.9 us -> 8.01 us  [the longest x3 5.08 us: on_device(): line = [lax.ppermute(ref_pair, plan, plane(s, True)) for s in (1, 2, 3)]]
    ppermute x13 -> x6, waiting for transfers between devices: 10.5 us -> 4.84 us  [the longest x3 3.56 us: on_device(): line = [lax.ppermute(ref_pair, plan, plane(s, True)) for s in (1, 2, 3)]]
    ppermute x5 -> x6, waiting for transfers between devices: 52.3 us -> 47.1 us  [on_device(): swap = lambda a: lax.ppermute(a, 'zl', PAIR)]
    all_to_all x1, blocking collectives: 21.6 us -> 25.5 us  [on_device(): lax.all_to_all(kept.reshape(4, 32, -1), 'zh', split_axis=0, concat_axis=0)]
    ppermute x5 -> x6, starting transfers between devices: 8.58 us -> 7.32 us  [on_device(): swap = lambda a: lax.ppermute(a, 'zl', PAIR)]
  transfers between devices with their start and end apart: 28 -> 22, of which waited for: 18 -> 14; matrix products, arithmetic and copies ran while one was open for 8% -> 8% of each run, Pallas kernels for 2% -> 0%
where the time goes in v3:
time: 195 us; the launch traced here: 194 us
  waiting for transfers between devices  71.4 us (37%)
  starting transfers between devices  46.3 us (24%)
  blocking collectives  43.4 us (22%)
  other arithmetic  14.3 us (7%)
  matrix products  9.22 us (5%)
  local copies, waits for them, and re-layouts  4.5 us (2%)
  Pallas kernels  3.73 us (2%)
    ppermute x6, waiting for transfers between devices, on_device(): swap = lambda a: lax.ppermute(a, 'zl', PAIR)  47.1 us
    all_to_all x1, blocking collectives, on_device(): lax.all_to_all(kept.reshape(4, 32, -1), 'zh', split_axis=0, concat_axis=0)  25.5 us
    all_to_all x3, starting transfers between devices, spread(): return lax.all_to_all(sent, axes, split_axis=0, concat_axis=0)  22.2 us
    all_to_all x1, blocking collectives, spread(): return lax.all_to_all(sent, axes, split_axis=0, concat_axis=0)  17.9 us
    all_to_all x3, waiting for transfers between devices, spread(): return lax.all_to_all(sent, axes, split_axis=0, concat_axis=0)  9.03 us
    ppermute x6, starting transfers between devices, on_device(): swap = lambda a: lax.ppermute(a, 'zl', PAIR)  7.32 us
    all_to_all x1, starting transfers between devices, on_device(): part = lax.all_to_all(part, img, split_axis=0, concat_axis=0)  6.65 us
    dot_general x2, matrix products, on_device(): lax.dot_general(a, refs, (((1,), (1,)), ((), ())), preferred_element_type...  5.26 us
  transfers between devices with their start and end apart: 22, of which 14 were waited for; matrix products, arithmetic and copies ran while one was open for 8% of the time, Pallas kernels for 0%

profile of v3, /device:TPU:56, one launch (start us, length us, event | category | flops | bytes accessed | tf_op | source)
XLA Modules:
  0.0 193.9 jit_solution(17224892120661598245)
XLA Ops:
  3.5 2.0 %collective-permute-start.3 = (bf16[48,1024]{1,0:T(8,128)(2,1)S(1)}, bf16[48,1024]{1,0:T(8,128)(2,1)S(1)}, u32[]{:S(2)}, u32[]{:S(2)}) collective-permute-start(bf16[48,1024]{1,0:T(8,128)(2,1)S(1)} %get-tuple-element.28), channel_id=1, source_target_pairs={{0,128},{128,0},{1,129},{129,1},{2,130},{130,2},{3,131},{131,3},{4... | collective-permute-start | bytes 294920 | tf_op jit(solution)/shard_map/ppermute | solution.py:65
  7.2 7.2 %all-to-all-start = ((f32[16,2,1024]{2,1,0:T(2,128)}), f32[16,2,1024]{2,1,0:T(2,128)S(1)}, u32[]{:S(2)}, u32[]{:S(2)}) async-start(f32[16,2,1024]{2,1,0:T(2,128)} %broadcast_in_dim.8), calls=%async_computation | async-start | bytes 262144 | tf_op jit(solution)/shard_map/all_to_all | solution.py:53
  15.0 3.1 %collective-permute-start.5 = (bf16[96,1024]{1,0:T(8,128)(2,1)S(1)}, bf16[96,1024]{1,0:T(8,128)(2,1)S(1)}, u32[]{:S(2)}, u32[]{:S(2)}) collective-permute-start(bf16[96,1024]{1,0:T(8,128)(2,1)S(1)} %get-tuple-element.26), channel_id=1, source_target_pairs={{0,64},{1,17},{8,72},{9,25},{16,80},{17,1},{24,88},{25,9},{32,96},... | collective-permute-start | bytes 589832 | tf_op jit(solution)/shard_map/ppermute | solution.py:75
  27.7 2.4 %collective-permute-start.8 = (bf16[4,96,1024]{2,1,0:T(8,128)(2,1)}, bf16[4,96,1024]{2,1,0:T(8,128)(2,1)}, u32[]{:S(2)}, u32[]{:S(2)}) collective-permute-start(bf16[4,96,1024]{2,1,0:T(8,128)(2,1)} %pad_maximum_fusion.refs_0_), channel_id=1, source_target_pairs={{0,16},{1,65},{8,24},{9,73},{16,0},{17,81},{24,8},{25,89},{32,48},... | collective-permute-start | bytes 2359304 | tf_op jit(solution)/shard_map/ppermute | solution.py:82
  30.7 9.5 %all-to-all-start.1 = ((f32[8,3,512]{2,1,0:T(4,128)}), f32[8,3,512]{2,1,0:T(4,128)S(1)}, u32[]{:S(2)}, u32[]{:S(2)}) async-start(f32[8,3,512]{2,1,0:T(4,128)} %broadcast_in_dim.9), calls=%async_computation.1 | async-start | bytes 131072 | tf_op jit(solution)/shard_map/all_to_all | solution.py:53
  40.4 6.7 %all-to-all-done.1 = f32[8,3,512]{2,1,0:T(4,128)S(1)} async-done(((f32[8,3,512]{2,1,0:T(4,128)}), f32[8,3,512]{2,1,0:T(4,128)S(1)}, u32[]{:S(2)}, u32[]{:S(2)}) %all-to-all-start.1) | async-done | bytes 49184 | tf_op jit(solution)/shard_map/all_to_all | solution.py:53
  49.9 3.7 %shard_map.67 = bf16[32,48,1024]{2,1,0:T(8,128)(2,1)} custom-call(s32[4]{0:T(128)} %pad_add_fusion.at, bf16[4,96,1024]{2,1,0:T(8,128)(2,1)} %pad_maximum_fusion.refs_0_, bf16[4,96,1024]{2,1,0:T(8,128)(2,1)} %collective-permute-done.7.refs_1_, bf16[4,96,1024]{2,1,0:T(8,128)(2,1)} %collective-permute-done.8.refs_2_, ...), custom_call_target="tpu_custom_call" | custom-call | tf_op jit(solution)/shard_map/pallas_call | solution.py:43
  53.7 2.7 %multiply_reduce_fusion = f32[32,48]{1,0:T(8,128)S(1)} fusion(bf16[32,48,1024]{2,1,0:T(8,128)(2,1)} %shard_map.67), kind=kLoop, calls=%fused_computation.1 | loop fusion | flops 4717056 | bytes 3151872 | tf_op jit(solution)/shard_map/reduce_sum | solution.py:112
  56.5 3.2 %convolution_subtract_fusion.1 = f32[256,1536]{1,0:T(8,128)} fusion(bf16[1536,1024]{1,0:T(8,128)(2,1)S(1)} %bitcast.67, f32[1536]{0:T(1024)S(1)} %mul.86, bf16[512,1024]{1,0:T(8,128)(2,1)} %fusion.4), kind=kOutput, calls=%fused_computation.4 | convolution fusion | flops 805699584 | bytes 5249024 | tf_op jit(solution)/shard_map/dot_general | solution.py:114
  59.7 2.1 %convolution_subtract_fusion = f32[256,1536]{1,0:T(8,128)S(1)} fusion(bf16[1536,1024]{1,0:T(8,128)(2,1)S(1)} %bitcast.68, f32[1536]{0:T(1024)S(1)} %mul.86, bf16[512,1024]{1,0:T(8,128)(2,1)} %fusion.4), kind=kOutput, calls=%fused_computation.3 | convolution fusion | flops 805699584 | bytes 5249024 | tf_op jit(solution)/shard_map/dot_general | solution.py:114
  65.3 2.0 %collective-permute-start.11 = (f32[128,768]{1,0:T(8,128)S(1)}, f32[128,768]{1,0:T(8,128)S(1)}, u32[]{:S(2)}, u32[]{:S(2)}) collective-permute-start(f32[128,768]{1,0:T(8,128)S(1)} %get-tuple-element.19), channel_id=1, source_target_pairs={{0,128},{128,0},{1,129},{129,1},{2,130},{130,2},{3,131},{131,3},{4... | collective-permute-start | bytes 1179656 | tf_op jit(solution)/shard_map/ppermute | solution.py:65
  67.3 1.9 collective-permute-start.12
  69.2 7.5 %collective-permute-done.11 = f32[128,768]{1,0:T(8,128)S(1)} collective-permute-done((f32[128,768]{1,0:T(8,128)S(1)}, f32[128,768]{1,0:T(8,128)S(1)}, u32[]{:S(2)}, u32[]{:S(2)}) %collective-permute-start.11) | collective-permute-done | bytes 393248 | tf_op jit(solution)/shard_map/ppermute | solution.py:65
  78.7 25.5 %all_to_all.30 = f32[4,32,1536]{2,1,0:T(8,128)S(1)} all-to-all(f32[4,32,1536]{2,1,0:T(8,128)S(1)} %maximum_add_fusion), channel_id=1, replica_groups=mesh['zl'=2,'x'=4,'y'=4,'zh'=4,'c'=2] {'zh'}, dimensions={0} | all-to-all | bytes 1572864 | tf_op jit(solution)/shard_map/all_to_all | solution.py:124
  105.3 17.9 %all_to_all.31 = bf16[4,32,1536]{2,1,0:T(8,128)(2,1)S(1)} all-to-all(bf16[4,32,1536]{2,1,0:T(8,128)(2,1)S(1)} %broadcast_in_dim.10), channel_id=1, replica_groups=mesh['zl'=2,'x'=4,'y'=4,'zh'=4,'c'=2] {'zh'}, dimensions={0} | all-to-all | bytes 786432 | tf_op jit(solution)/shard_map/all_to_all | solution.py:53
  123.2 2.4 %collective-permute-start.13 = (bf16[128,768]{1,0:T(8,128)(2,1)S(1)}, bf16[128,768]{1,0:T(8,128)(2,1)S(1)}, u32[]{:S(2)}, u32[]{:S(2)}) collective-permute-start(bf16[128,768]{1,0:T(8,128)(2,1)S(1)} %get-tuple-element.24), channel_id=1, source_target_pairs={{0,128},{128,0},{1,129},{129,1},{2,130},{130,2},{3,131},{131,3},{4... | collective-permute-start | bytes 589832 | tf_op jit(solution)/shard_map/ppermute | solution.py:65
  125.6 3.6 %collective-permute-done.13 = bf16[128,768]{1,0:T(8,128)(2,1)S(1)} collective-permute-done((bf16[128,768]{1,0:T(8,128)(2,1)S(1)}, bf16[128,768]{1,0:T(8,128)(2,1)S(1)}, u32[]{:S(2)}, u32[]{:S(2)}) %collective-permute-start.13) | collective-permute-done | bytes 196640 | tf_op jit(solution)/shard_map/ppermute | solution.py:65
  129.3 2.0 %collective-permute-done.14 = bf16[128,768]{1,0:T(8,128)(2,1)S(1)} collective-permute-done((bf16[128,768]{1,0:T(8,128)(2,1)S(1)}, bf16[128,768]{1,0:T(8,128)(2,1)S(1)}, u32[]{:S(2)}, u32[]{:S(2)}) %collective-permute-start.14) | collective-permute-done | bytes 196640 | tf_op jit(solution)/shard_map/ppermute | solution.py:66
  132.8 5.6 %all-to-all-start.5 = ((f32[16,1,96]{2,1,0:T(1,128)}), f32[16,1,96]{2,1,0:T(1,128)S(1)}, u32[]{:S(2)}, u32[]{:S(2)}) async-start(f32[16,1,96]{2,1,0:T(1,128)} %broadcast_in_dim.11), calls=%async_computation.5 | async-start | bytes 16384 | tf_op jit(solution)/shard_map/all_to_all | solution.py:53
  138.4 3.5 %convolution_convert_fusion = bf16[1536,1024]{1,0:T(8,128)(2,1)} fusion(bf16[512,1024]{1,0:T(8,128)(2,1)S(1)} %copy-done.2, bf16[256,1536]{1,0:T(8,128)(2,1)S(1)} %collective-permute-done.15, bf16[256,1536]{1,0:T(8,128)(2,1)S(1)} %maximum_select_fusion.2), kind=kOutput, calls=%fused_computation.2 | convolution fusion | flops 1615331328 | bytes 5767168 | tf_op jit(solution)/shard_map/dot_general | solution.py:148
  141.9 2.1 %all-to-all-done.5 = f32[16,1,96]{2,1,0:T(1,128)S(1)} async-done(((f32[16,1,96]{2,1,0:T(1,128)}), f32[16,1,96]{2,1,0:T(1,128)S(1)}, u32[]{:S(2)}, u32[]{:S(2)}) %all-to-all-start.5) | async-done | bytes 6176 | tf_op jit(solution)/shard_map/all_to_all | solution.py:53
  143.9 6.6 %all-to-all-start.4 = ((bf16[32,48,1024]{2,1,0:T(8,128)(2,1)}), bf16[32,48,1024]{2,1,0:T(8,128)(2,1)S(1)}, u32[]{:S(2)}, u32[]{:S(2)}) async-start(bf16[32,48,1024]{2,1,0:T(8,128)(2,1)} %bitcast.72), calls=%async_computation.4 | async-start | bytes 6291456 | tf_op jit(solution)/shard_map/all_to_all | solution.py:150
  151.2 36.0 %collective-permute-done.16 = f32[1,96]{1,0:T(1,128)S(1)} collective-permute-done((f32[1,96]{1,0:T(1,128)S(1)}, f32[1,96]{1,0:T(1,128)S(1)}, u32[]{:S(2)}, u32[]{:S(2)}) %collective-permute-start.16) | collective-permute-done | bytes 416 | tf_op jit(solution)/shard_map/ppermute | solution.py:65
  188.8 3.7 %all-to-all-done.4 = bf16[32,48,1024]{2,1,0:T(8,128)(2,1)S(1)} async-done(((bf16[32,48,1024]{2,1,0:T(8,128)(2,1)}), bf16[32,48,1024]{2,1,0:T(8,128)(2,1)S(1)}, u32[]{:S(2)}, u32[]{:S(2)}) %all-to-all-start.4) | async-done | bytes 3145760 | tf_op jit(solution)/shard_map/all_to_all | solution.py:150
  (98 shorter events, 30.1 us)
Async XLA Ops:
  2.4 4.1 %collective-permute-start.1 = (f32[2,1024]{1,0:T(2,128)S(1)}, f32[2,1024]{1,0:T(2,128)S(1)}, u32[]{:S(2)}, u32[]{:S(2)}) collective-permute-start(f32[2,1024]{1,0:T(2,128)S(1)} %fusion.12), channel_id=1, source_target_pairs={{0,128},{128,0},{1,129},{129,1},{2,130},{130,2},{3,131},{131,3},{4... | collective-permute-start | bytes 24584 | tf_op jit(solution)/shard_map/ppermute | solution.py:65
  3.5 11.5 %collective-permute-start.3 = (bf16[48,1024]{1,0:T(8,128)(2,1)S(1)}, bf16[48,1024]{1,0:T(8,128)(2,1)S(1)}, u32[]{:S(2)}, u32[]{:S(2)}) collective-permute-start(bf16[48,1024]{1,0:T(8,128)(2,1)S(1)} %get-tuple-element.28), channel_id=1, source_target_pairs={{0,128},{128,0},{1,129},{129,1},{2,130},{130,2},{3,131},{131,3},{4... | collective-permute-start | bytes 294920 | tf_op jit(solution)/shard_map/ppermute | solution.py:65
  5.6 14.9 %collective-permute-start = (bf16[256,1024]{1,0:T(8,128)(2,1)S(1)}, bf16[256,1024]{1,0:T(8,128)(2,1)S(1)}, u32[]{:S(2)}, u32[]{:S(2)}) collective-permute-start(bf16[256,1024]{1,0:T(8,128)(2,1)S(1)} %get-tuple-element.18), channel_id=1, source_target_pairs={{0,128},{128,0},{1,129},{129,1},{2,130},{130,2},{3,131},{131,3},{4... | collective-permute-start | bytes 1572872 | tf_op jit(solution)/shard_map/ppermute | solution.py:65
  7.2 13.2 %all-to-all-start = ((f32[16,2,1024]{2,1,0:T(2,128)}), f32[16,2,1024]{2,1,0:T(2,128)S(1)}, u32[]{:S(2)}, u32[]{:S(2)}) async-start(f32[16,2,1024]{2,1,0:T(2,128)} %broadcast_in_dim.8), calls=%async_computation | async-start | bytes 262144 | tf_op jit(solution)/shard_map/all_to_all | solution.py:53
  15.0 7.5 %collective-permute-start.5 = (bf16[96,1024]{1,0:T(8,128)(2,1)S(1)}, bf16[96,1024]{1,0:T(8,128)(2,1)S(1)}, u32[]{:S(2)}, u32[]{:S(2)}) collective-permute-start(bf16[96,1024]{1,0:T(8,128)(2,1)S(1)} %get-tuple-element.26), channel_id=1, source_target_pairs={{0,64},{1,17},{8,72},{9,25},{16,80},{17,1},{24,88},{25,9},{32,96},... | collective-permute-start | bytes 589832 | tf_op jit(solution)/shard_map/ppermute | solution.py:75
  18.1 6.3 %collective-permute-start.4 = (bf16[96,1024]{1,0:T(8,128)(2,1)S(1)}, bf16[96,1024]{1,0:T(8,128)(2,1)S(1)}, u32[]{:S(2)}, u32[]{:S(2)}) collective-permute-start(bf16[96,1024]{1,0:T(8,128)(2,1)S(1)} %get-tuple-element.26), channel_id=1, source_target_pairs={{0,96},{1,25},{8,104},{9,1},{16,112},{17,9},{24,120},{25,17},{32,0... | collective-permute-start | bytes 589832 | tf_op jit(solution)/shard_map/ppermute | solution.py:75
  19.3 6.9 %collective-permute-start.6 = (bf16[96,1024]{1,0:T(8,128)(2,1)S(1)}, bf16[96,1024]{1,0:T(8,128)(2,1)S(1)}, u32[]{:S(2)}, u32[]{:S(2)}) collective-permute-start(bf16[96,1024]{1,0:T(8,128)(2,1)S(1)} %get-tuple-element.26), channel_id=1, source_target_pairs={{0,32},{1,9},{8,40},{9,17},{16,48},{17,25},{24,56},{25,1},{32,64},... | collective-permute-start | bytes 589832 | tf_op jit(solution)/shard_map/ppermute | solution.py:75
  22.5 7.6 %collective-permute-start.2 = (f32[3,512]{1,0:T(4,128)S(1)}, f32[3,512]{1,0:T(4,128)S(1)}, u32[]{:S(2)}, u32[]{:S(2)}) collective-permute-start(f32[3,512]{1,0:T(4,128)S(1)} %bitcast.89), channel_id=1, source_target_pairs={{0,1},{1,0},{2,3},{3,2},{4,5},{5,4},{6,7},{7,6},{8,9},{9,8},{10,11... | collective-permute-start | bytes 18440 | tf_op jit(solution)/shard_map/ppermute | solution.py:100
  27.1 21.5 %collective-permute-start.9 = (bf16[4,96,1024]{2,1,0:T(8,128)(2,1)}, bf16[4,96,1024]{2,1,0:T(8,128)(2,1)}, u32[]{:S(2)}, u32[]{:S(2)}) collective-permute-start(bf16[4,96,1024]{2,1,0:T(8,128)(2,1)} %pad_maximum_fusion.refs_0_), channel_id=1, source_target_pairs={{0,8},{1,33},{8,16},{9,41},{16,24},{17,49},{24,0},{25,57},{32,40},... | collective-permute-start | bytes 2359304 | tf_op jit(solution)/shard_map/ppermute | solution.py:82
  27.7 21.0 %collective-permute-start.8 = (bf16[4,96,1024]{2,1,0:T(8,128)(2,1)}, bf16[4,96,1024]{2,1,0:T(8,128)(2,1)}, u32[]{:S(2)}, u32[]{:S(2)}) collective-permute-start(bf16[4,96,1024]{2,1,0:T(8,128)(2,1)} %pad_maximum_fusion.refs_0_), channel_id=1, source_target_pairs={{0,16},{1,65},{8,24},{9,73},{16,0},{17,81},{24,8},{25,89},{32,48},... | collective-permute-start | bytes 2359304 | tf_op jit(solution)/shard_map/ppermute | solution.py:82
  30.0 19.9 %collective-permute-start.7 = (bf16[4,96,1024]{2,1,0:T(8,128)(2,1)}, bf16[4,96,1024]{2,1,0:T(8,128)(2,1)}, u32[]{:S(2)}, u32[]{:S(2)}) collective-permute-start(bf16[4,96,1024]{2,1,0:T(8,128)(2,1)} %pad_maximum_fusion.refs_0_), channel_id=1, source_target_pairs={{0,24},{1,97},{8,0},{9,105},{16,8},{17,113},{24,16},{25,121},{32,5... | collective-permute-start | bytes 2359304 | tf_op jit(solution)/shard_map/ppermute | solution.py:82
  30.7 16.4 %all-to-all-start.1 = ((f32[8,3,512]{2,1,0:T(4,128)}), f32[8,3,512]{2,1,0:T(4,128)S(1)}, u32[]{:S(2)}, u32[]{:S(2)}) async-start(f32[8,3,512]{2,1,0:T(4,128)} %broadcast_in_dim.9), calls=%async_computation.1 | async-start | bytes 131072 | tf_op jit(solution)/shard_map/all_to_all | solution.py:53
  59.7 3.8 %collective-permute-start.10 = (f32[256,1536]{1,0:T(8,128)}, f32[256,1536]{1,0:T(8,128)}, u32[]{:S(2)}, u32[]{:S(2)}) collective-permute-start(f32[256,1536]{1,0:T(8,128)} %convolution_subtract_fusion.1), channel_id=1, source_target_pairs={{0,1},{1,0},{2,3},{3,2},{4,5},{5,4},{6,7},{7,6},{8,9},{9,8},{10,11... | collective-permute-start | bytes 4718600 | tf_op jit(solution)/shard_map/ppermute | solution.py:117
  65.3 11.4 %collective-permute-start.11 = (f32[128,768]{1,0:T(8,128)S(1)}, f32[128,768]{1,0:T(8,128)S(1)}, u32[]{:S(2)}, u32[]{:S(2)}) collective-permute-start(f32[128,768]{1,0:T(8,128)S(1)} %get-tuple-element.19), channel_id=1, source_target_pairs={{0,128},{128,0},{1,129},{129,1},{2,130},{130,2},{3,131},{131,3},{4... | collective-permute-start | bytes 1179656 | tf_op jit(solution)/shard_map/ppermute | solution.py:65
  67.3 11.3 %collective-permute-start.12 = (f32[128,768]{1,0:T(8,128)S(1)}, f32[128,768]{1,0:T(8,128)S(1)}, u32[]{:S(2)}, u32[]{:S(2)}) collective-permute-start(f32[128,768]{1,0:T(8,128)S(1)} %get-tuple-element.20), channel_id=1, source_target_pairs={{0,134},{2,128},{4,130},{6,132},{128,2},{130,4},{132,6},{134,0},{1... | collective-permute-start | bytes 1179656 | tf_op jit(solution)/shard_map/ppermute | solution.py:66
  105.3 26.4 %copy-start.4 = (s32[1536]{0:T(1024)S(1)}, s32[1536]{0:T(1024)}, u32[]{:S(2)}) copy-start(s32[1536]{0:T(1024)} %param.7) | copy-start | bytes 18436
  123.2 15.2 %copy-start.2 = (bf16[512,1024]{1,0:T(8,128)(2,1)S(1)}, bf16[512,1024]{1,0:T(8,128)(2,1)}, u32[]{:S(2)}) copy-start(bf16[512,1024]{1,0:T(8,128)(2,1)} %fusion.4) | copy-start | bytes 3145732
  123.2 6.0 %collective-permute-start.13 = (bf16[128,768]{1,0:T(8,128)(2,1)S(1)}, bf16[128,768]{1,0:T(8,128)(2,1)S(1)}, u32[]{:S(2)}, u32[]{:S(2)}) collective-permute-start(bf16[128,768]{1,0:T(8,128)(2,1)S(1)} %get-tuple-element.24), channel_id=1, source_target_pairs={{0,128},{128,0},{1,129},{129,1},{2,130},{130,2},{3,131},{131,3},{4... | collective-permute-start | bytes 589832 | tf_op jit(solution)/shard_map/ppermute | solution.py:65
  125.6 5.7 %collective-permute-start.14 = (bf16[128,768]{1,0:T(8,128)(2,1)S(1)}, bf16[128,768]{1,0:T(8,128)(2,1)S(1)}, u32[]{:S(2)}, u32[]{:S(2)}) collective-permute-start(bf16[128,768]{1,0:T(8,128)(2,1)S(1)} %get-tuple-element.23), channel_id=1, source_target_pairs={{0,134},{2,128},{4,130},{6,132},{128,2},{130,4},{132,6},{134,0},{1... | collective-permute-start | bytes 589832 | tf_op jit(solution)/shard_map/ppermute | solution.py:66
  131.5 6.9 %collective-permute-start.15 = (bf16[256,1536]{1,0:T(8,128)(2,1)S(1)}, bf16[256,1536]{1,0:T(8,128)(2,1)S(1)}, u32[]{:S(2)}, u32[]{:S(2)}) collective-permute-start(bf16[256,1536]{1,0:T(8,128)(2,1)S(1)} %maximum_select_fusion.2), channel_id=1, source_target_pairs={{0,1},{1,0},{2,3},{3,2},{4,5},{5,4},{6,7},{7,6},{8,9},{9,8},{10,11... | collective-permute-start | bytes 2359304 | tf_op jit(solution)/shard_map/ppermute | solution.py:143
  132.8 11.1 %all-to-all-start.5 = ((f32[16,1,96]{2,1,0:T(1,128)}), f32[16,1,96]{2,1,0:T(1,128)S(1)}, u32[]{:S(2)}, u32[]{:S(2)}) async-start(f32[16,1,96]{2,1,0:T(1,128)} %broadcast_in_dim.11), calls=%async_computation.5 | async-start | bytes 16384 | tf_op jit(solution)/shard_map/all_to_all | solution.py:53
  143.9 48.5 %all-to-all-start.4 = ((bf16[32,48,1024]{2,1,0:T(8,128)(2,1)}), bf16[32,48,1024]{2,1,0:T(8,128)(2,1)S(1)}, u32[]{:S(2)}, u32[]{:S(2)}) async-start(bf16[32,48,1024]{2,1,0:T(8,128)(2,1)} %bitcast.72), calls=%async_computation.4 | async-start | bytes 6291456 | tf_op jit(solution)/shard_map/all_to_all | solution.py:150
  150.6 36.5 %collective-permute-start.16 = (f32[1,96]{1,0:T(1,128)S(1)}, f32[1,96]{1,0:T(1,128)S(1)}, u32[]{:S(2)}, u32[]{:S(2)}) collective-permute-start(f32[1,96]{1,0:T(1,128)S(1)} %bitcast.95), channel_id=1, source_target_pairs={{0,128},{128,0},{1,129},{129,1},{2,130},{130,2},{3,131},{131,3},{4... | collective-permute-start | bytes 1160 | tf_op jit(solution)/shard_map/ppermute | solution.py:65
  187.1 1.2 collective-permute-start.17
  (3 other events, 12.9 us)

commit v4 on v3

--- a/solution.py
+++ b/solution.py
@@ -54,7 +54,7 @@
 
 
 def on_device(images, references, cycle_mask, view_class):
-    zl, x, y, core = (lax.axis_index(a) for a in ("zl", "x", "y", "c"))
+    zl, x, y, zh, core = (lax.axis_index(a) for a in ("zl", "x", "y", "zh", "c"))
     rows, wide = images.shape
     half = wide // 2
     views = references.shape[0]
@@ -121,8 +121,18 @@
     kept = lax.dynamic_index_in_dim(both, zl, 0, False)
     sent = lax.dynamic_index_in_dim(both, 1 - zl, 0, False)
     kept = kept + jnp.concatenate([swap(sent[:, :cut]), far(sent[:, cut:])], 1)
-    pieces = lax.all_to_all(kept.reshape(4, 32, -1), "zh", split_axis=0, concat_axis=0)
-    scores = jnp.sum(pieces, 0) * (4.0 / SIDE)
+    up = lambda a: lax.ppermute(a, "zh", [(i, (i + 1) % 4) for i in range(4)])
+    down = lambda a: lax.ppermute(a, "zh", [((i + 1) % 4, i) for i in range(4)])
+    take = lambda step, skip, count: lax.dynamic_slice_in_dim(
+        kept, (zh + step) % 4 * 32 + skip, count
+    )
+    pass_up, pass_down = lax.optimization_barrier((take(2, 0, 16), take(2, 16, 16)))
+    came_up, came_down = lax.optimization_barrier((up(pass_up), down(pass_down)))
+    to_next = jnp.concatenate([take(1, 0, 16) + came_up, take(1, 16, 16)])
+    to_last = jnp.concatenate([take(3, 0, 16), take(3, 16, 16) + came_down])
+    to_next, to_last = lax.optimization_barrier((to_next, to_last))
+    came_up, came_down = lax.optimization_barrier((up(to_next), down(to_last)))
+    scores = (take(0, 0, 32) + came_up + came_down) * (4.0 / SIDE)
 
     row_max = jnp.max(scores, 1, keepdims=True)
     log_total = row_max[:, 0] + jnp.log(jnp.sum(jnp.exp(scores - row_max), 1))

time: 195 us -> 201 us (1.031)
  blocking collectives: 43.4 us -> 14.1 us
  waiting for transfers between devices: 71.4 us -> 98.3 us
  starting transfers between devices: 46.3 us -> 55.7 us
    all_to_all x1 -> x0, blocking collectives: 25.5 us -> none  [on_device(): lax.all_to_all(kept.reshape(4, 32, -1), 'zh', split_axis=0, concat_axis=0)]
    ppermute x0 -> x4, waiting for transfers between devices: none -> 14.2 us  [the longest x2 10.9 us: on_device(): up = lambda a: lax.ppermute(a, 'zh', [(i, (i + 1) % 4) for i in range(4)])]
    ppermute x6, waiting for transfers between devices: 47.1 us -> 59 us  [on_device(): swap = lambda a: lax.ppermute(a, 'zl', PAIR)]
    ppermute x0 -> x4, starting transfers between devices: none -> 9.91 us  [the longest x2 7.8 us: on_device(): up = lambda a: lax.ppermute(a, 'zh', [(i, (i + 1) % 4) for i in range(4)])]
    all_to_all x1, blocking collectives: 17.9 us -> 14.1 us  [spread(): return lax.all_to_all(sent, axes, split_axis=0, concat_axis=0)]
  transfers between devices with their start and end apart: 22 -> 26, of which waited for: 14 -> 21; matrix products, arithmetic and copies ran while one was open for 8% -> 8% of each run, Pallas kernels for 0% -> 0%
where the time goes in v4:
time: 201 us
  waiting for transfers between devices  98.3 us (49%)
  starting transfers between devices  55.7 us (28%)
  blocking collectives  14.1 us (7%)
  other arithmetic  13 us (6%)
  matrix products  9.18 us (5%)
  local copies, waits for them, and re-layouts  5.74 us (3%)
  Pallas kernels  3.7 us (2%)
    ppermute x6, waiting for transfers between devices, on_device(): swap = lambda a: lax.ppermute(a, 'zl', PAIR)  59 us
    all_to_all x3, starting transfers between devices, spread(): return lax.all_to_all(sent, axes, split_axis=0, concat_axis=0)  20.8 us
    all_to_all x1, blocking collectives, spread(): return lax.all_to_all(sent, axes, split_axis=0, concat_axis=0)  14.1 us
    ppermute x2, waiting for transfers between devices, on_device(): up = lambda a: lax.ppermute(a, 'zh', [(i, (i + 1) % 4) for i in range(4)])  10.9 us
    all_to_all x3, waiting for transfers between devices, spread(): return lax.all_to_all(sent, axes, split_axis=0, concat_axis=0)  9.7 us
    all_to_all x1, starting transfers between devices, on_device(): part = lax.all_to_all(part, img, split_axis=0, concat_axis=0)  7.91 us
    ppermute x2, starting transfers between devices, on_device(): up = lambda a: lax.ppermute(a, 'zh', [(i, (i + 1) % 4) for i in range(4)])  7.8 us
    ppermute x6, starting transfers between devices, on_device(): swap = lambda a: lax.ppermute(a, 'zl', PAIR)  5.42 us
  transfers between devices with their start and end apart: 26, of which 21 were waited for; matrix products, arithmetic and copies ran while one was open for 8% of the time, Pallas kernels for 0%

profile of v4, /device:TPU:56, one launch (start us, length us, event | category | flops | bytes accessed | tf_op | source)
XLA Modules:
  0.0 200.7 jit_solution(2662488410964878001)
XLA Ops:
  6.4 11.4 %collective-permute-done.1 = f32[2,1024]{1,0:T(2,128)S(1)} collective-permute-done((f32[2,1024]{1,0:T(2,128)S(1)}, f32[2,1024]{1,0:T(2,128)S(1)}, u32[]{:S(2)}, u32[]{:S(2)}) %collective-permute-start.1) | collective-permute-done | bytes 8224 | tf_op jit(solution)/shard_map/ppermute | solution.py:65
  18.6 7.2 %all-to-all-start = ((f32[16,2,1024]{2,1,0:T(2,128)}), f32[16,2,1024]{2,1,0:T(2,128)S(1)}, u32[]{:S(2)}, u32[]{:S(2)}) async-start(f32[16,2,1024]{2,1,0:T(2,128)} %broadcast_in_dim.8), calls=%async_computation | async-start | bytes 262144 | tf_op jit(solution)/shard_map/all_to_all | solution.py:53
  26.4 2.8 %collective-permute-start.4 = (bf16[96,1024]{1,0:T(8,128)(2,1)S(1)}, bf16[96,1024]{1,0:T(8,128)(2,1)S(1)}, u32[]{:S(2)}, u32[]{:S(2)}) collective-permute-start(bf16[96,1024]{1,0:T(8,128)(2,1)S(1)} %get-tuple-element.48), channel_id=1, source_target_pairs={{0,96},{1,25},{8,104},{9,1},{16,112},{17,9},{24,120},{25,17},{32,0... | collective-permute-start | bytes 589832 | tf_op jit(solution)/shard_map/ppermute | solution.py:75
  41.4 2.1 %collective-permute-start.9 = (bf16[4,96,1024]{2,1,0:T(8,128)(2,1)}, bf16[4,96,1024]{2,1,0:T(8,128)(2,1)}, u32[]{:S(2)}, u32[]{:S(2)}) collective-permute-start(bf16[4,96,1024]{2,1,0:T(8,128)(2,1)} %pad_maximum_fusion.refs_0_), channel_id=1, source_target_pairs={{0,8},{1,33},{8,16},{9,41},{16,24},{17,49},{24,0},{25,57},{32,40},... | collective-permute-start | bytes 2359304 | tf_op jit(solution)/shard_map/ppermute | solution.py:82
  44.1 8.6 %all-to-all-start.1 = ((f32[8,3,512]{2,1,0:T(4,128)}), f32[8,3,512]{2,1,0:T(4,128)S(1)}, u32[]{:S(2)}, u32[]{:S(2)}) async-start(f32[8,3,512]{2,1,0:T(4,128)} %broadcast_in_dim.9), calls=%async_computation.1 | async-start | bytes 131072 | tf_op jit(solution)/shard_map/all_to_all | solution.py:53
  52.9 6.7 %all-to-all-done.1 = f32[8,3,512]{2,1,0:T(4,128)S(1)} async-done(((f32[8,3,512]{2,1,0:T(4,128)}), f32[8,3,512]{2,1,0:T(4,128)S(1)}, u32[]{:S(2)}, u32[]{:S(2)}) %all-to-all-start.1) | async-done | bytes 49184 | tf_op jit(solution)/shard_map/all_to_all | solution.py:53
  62.2 3.7 %shard_map.67 = bf16[32,48,1024]{2,1,0:T(8,128)(2,1)} custom-call(s32[4]{0:T(128)} %pad_add_fusion.at, bf16[4,96,1024]{2,1,0:T(8,128)(2,1)} %pad_maximum_fusion.refs_0_, bf16[4,96,1024]{2,1,0:T(8,128)(2,1)} %collective-permute-done.7.refs_1_, bf16[4,96,1024]{2,1,0:T(8,128)(2,1)} %collective-permute-done.8.refs_2_, ...), custom_call_target="tpu_custom_call" | custom-call | tf_op jit(solution)/shard_map/pallas_call | solution.py:43
  65.9 2.7 %multiply_reduce_fusion = f32[32,48]{1,0:T(8,128)S(1)} fusion(bf16[32,48,1024]{2,1,0:T(8,128)(2,1)} %shard_map.67), kind=kLoop, calls=%fused_computation.1 | loop fusion | flops 4717056 | bytes 3151872 | tf_op jit(solution)/shard_map/reduce_sum | solution.py:112
  68.8 3.2 %convolution_subtract_fusion.1 = f32[256,1536]{1,0:T(8,128)} fusion(bf16[1536,1024]{1,0:T(8,128)(2,1)S(1)} %bitcast.66, f32[1536]{0:T(1024)S(1)} %mul.97, bf16[512,1024]{1,0:T(8,128)(2,1)} %fusion.4), kind=kOutput, calls=%fused_computation.4 | convolution fusion | flops 805699584 | bytes 5249024 | tf_op jit(solution)/shard_map/dot_general | solution.py:114
  78.5 2.9 %collective-permute-start.12 = (f32[128,768]{1,0:T(8,128)S(1)}, f32[128,768]{1,0:T(8,128)S(1)}, u32[]{:S(2)}, u32[]{:S(2)}) collective-permute-start(f32[128,768]{1,0:T(8,128)S(1)} %get-tuple-element.42), channel_id=1, source_target_pairs={{0,134},{2,128},{4,130},{6,132},{128,2},{130,4},{132,6},{134,0},{1... | collective-permute-start | bytes 1179656 | tf_op jit(solution)/shard_map/ppermute | solution.py:66
  81.4 7.3 %collective-permute-done.11 = f32[128,768]{1,0:T(8,128)S(1)} collective-permute-done((f32[128,768]{1,0:T(8,128)S(1)}, f32[128,768]{1,0:T(8,128)S(1)}, u32[]{:S(2)}, u32[]{:S(2)}) %collective-permute-start.11) | collective-permute-done | bytes 393248 | tf_op jit(solution)/shard_map/ppermute | solution.py:65
  90.7 3.7 %collective-permute-start.13 = (f32[16,1536]{1,0:T(8,128)S(1)}, f32[16,1536]{1,0:T(8,128)S(1)}, u32[]{:S(2)}, u32[]{:S(2)}) collective-permute-start(f32[16,1536]{1,0:T(8,128)S(1)} %get-tuple-element.11), channel_id=1, source_target_pairs={{0,2},{2,4},{4,6},{6,0},{1,3},{3,5},{5,7},{7,1},{8,10},{10,12},{12... | collective-permute-start | bytes 294920 | tf_op jit(solution)/shard_map/ppermute | solution.py:124
  96.4 3.1 %collective-permute-done.13 = f32[16,1536]{1,0:T(8,128)S(1)} collective-permute-done((f32[16,1536]{1,0:T(8,128)S(1)}, f32[16,1536]{1,0:T(8,128)S(1)}, u32[]{:S(2)}, u32[]{:S(2)}) %collective-permute-start.13) | collective-permute-done | bytes 98336 | tf_op jit(solution)/shard_map/ppermute | solution.py:124
  100.0 4.1 %collective-permute-start.15 = (f32[32,1536]{1,0:T(8,128)S(1)}, f32[32,1536]{1,0:T(8,128)S(1)}, u32[]{:S(2)}, u32[]{:S(2)}) collective-permute-start(f32[32,1536]{1,0:T(8,128)S(1)} %get-tuple-element.15), channel_id=1, source_target_pairs={{0,2},{2,4},{4,6},{6,0},{1,3},{3,5},{5,7},{7,1},{8,10},{10,12},{12... | collective-permute-start | bytes 589832 | tf_op jit(solution)/shard_map/ppermute | solution.py:124
  104.2 7.9 %collective-permute-done.15 = f32[32,1536]{1,0:T(8,128)S(1)} collective-permute-done((f32[32,1536]{1,0:T(8,128)S(1)}, f32[32,1536]{1,0:T(8,128)S(1)}, u32[]{:S(2)}, u32[]{:S(2)}) %collective-permute-start.15) | collective-permute-done | bytes 196640 | tf_op jit(solution)/shard_map/ppermute | solution.py:124
  112.1 2.7 %collective-permute-done.16 = f32[32,1536]{1,0:T(8,128)S(1)} collective-permute-done((f32[32,1536]{1,0:T(8,128)S(1)}, f32[32,1536]{1,0:T(8,128)S(1)}, u32[]{:S(2)}, u32[]{:S(2)}) %collective-permute-start.16) | collective-permute-done | bytes 196640 | tf_op jit(solution)/shard_map/ppermute | solution.py:125
  115.9 14.1 %all_to_all.25 = bf16[4,32,1536]{2,1,0:T(8,128)(2,1)S(1)} all-to-all(bf16[4,32,1536]{2,1,0:T(8,128)(2,1)S(1)} %broadcast_in_dim.10), channel_id=1, replica_groups=mesh['zl'=2,'x'=4,'y'=4,'zh'=4,'c'=2] {'zh'}, dimensions={0} | all-to-all | bytes 786432 | tf_op jit(solution)/shard_map/all_to_all | solution.py:53
  131.5 4.3 %collective-permute-done.17 = bf16[128,768]{1,0:T(8,128)(2,1)S(1)} collective-permute-done((bf16[128,768]{1,0:T(8,128)(2,1)S(1)}, bf16[128,768]{1,0:T(8,128)(2,1)S(1)}, u32[]{:S(2)}, u32[]{:S(2)}) %collective-permute-start.17) | collective-permute-done | bytes 196640 | tf_op jit(solution)/shard_map/ppermute | solution.py:65
  138.6 5.1 %all-to-all-start.4 = ((f32[16,1,96]{2,1,0:T(1,128)}), f32[16,1,96]{2,1,0:T(1,128)S(1)}, u32[]{:S(2)}, u32[]{:S(2)}) async-start(f32[16,1,96]{2,1,0:T(1,128)} %broadcast_in_dim.11), calls=%async_computation.4 | async-start | bytes 16384 | tf_op jit(solution)/shard_map/all_to_all | solution.py:53
  143.7 3.5 %convolution_convert_fusion = bf16[1536,1024]{1,0:T(8,128)(2,1)} fusion(bf16[512,1024]{1,0:T(8,128)(2,1)S(1)} %copy-done.2, bf16[256,1536]{1,0:T(8,128)(2,1)S(1)} %collective-permute-done.19, bf16[256,1536]{1,0:T(8,128)(2,1)S(1)} %maximum_select_fusion.2), kind=kOutput, calls=%fused_computation.2 | convolution fusion | flops 1615331328 | bytes 5767168 | tf_op jit(solution)/shard_map/dot_general | solution.py:158
  147.2 2.1 %all-to-all-done.4 = f32[16,1,96]{2,1,0:T(1,128)S(1)} async-done(((f32[16,1,96]{2,1,0:T(1,128)}), f32[16,1,96]{2,1,0:T(1,128)S(1)}, u32[]{:S(2)}, u32[]{:S(2)}) %all-to-all-start.4) | async-done | bytes 6176 | tf_op jit(solution)/shard_map/all_to_all | solution.py:53
  149.3 7.9 %all-to-all-start.3 = ((bf16[32,48,1024]{2,1,0:T(8,128)(2,1)}), bf16[32,48,1024]{2,1,0:T(8,128)(2,1)S(1)}, u32[]{:S(2)}, u32[]{:S(2)}) async-start(bf16[32,48,1024]{2,1,0:T(8,128)(2,1)} %bitcast.72), calls=%async_computation.3 | async-start | bytes 6291456 | tf_op jit(solution)/shard_map/all_to_all | solution.py:160
  157.7 36.0 %collective-permute-done.20 = f32[1,96]{1,0:T(1,128)S(1)} collective-permute-done((f32[1,96]{1,0:T(1,128)S(1)}, f32[1,96]{1,0:T(1,128)S(1)}, u32[]{:S(2)}, u32[]{:S(2)}) %collective-permute-start.20) | collective-permute-done | bytes 416 | tf_op jit(solution)/shard_map/ppermute | solution.py:65
  195.4 3.8 %all-to-all-done.3 = bf16[32,48,1024]{2,1,0:T(8,128)(2,1)S(1)} async-done(((bf16[32,48,1024]{2,1,0:T(8,128)(2,1)}), bf16[32,48,1024]{2,1,0:T(8,128)(2,1)S(1)}, u32[]{:S(2)}, u32[]{:S(2)}) %all-to-all-start.3) | async-done | bytes 3145760 | tf_op jit(solution)/shard_map/all_to_all | solution.py:160
  (107 shorter events, 43.0 us)
Async XLA Ops:
  1.7 24.6 %collective-permute-start.3 = (bf16[48,1024]{1,0:T(8,128)(2,1)S(1)}, bf16[48,1024]{1,0:T(8,128)(2,1)S(1)}, u32[]{:S(2)}, u32[]{:S(2)}) collective-permute-start(bf16[48,1024]{1,0:T(8,128)(2,1)S(1)} %get-tuple-element.50), channel_id=1, source_target_pairs={{0,128},{128,0},{1,129},{129,1},{2,130},{130,2},{3,131},{131,3},{4... | collective-permute-start | bytes 294920 | tf_op jit(solution)/shard_map/ppermute | solution.py:65
  3.2 28.6 %collective-permute-start = (bf16[256,1024]{1,0:T(8,128)(2,1)S(1)}, bf16[256,1024]{1,0:T(8,128)(2,1)S(1)}, u32[]{:S(2)}, u32[]{:S(2)}) collective-permute-start(bf16[256,1024]{1,0:T(8,128)(2,1)S(1)} %get-tuple-element.34), channel_id=1, source_target_pairs={{0,128},{128,0},{1,129},{129,1},{2,130},{130,2},{3,131},{131,3},{4... | collective-permute-start | bytes 1572872 | tf_op jit(solution)/shard_map/ppermute | solution.py:65
  5.6 12.2 %collective-permute-start.1 = (f32[2,1024]{1,0:T(2,128)S(1)}, f32[2,1024]{1,0:T(2,128)S(1)}, u32[]{:S(2)}, u32[]{:S(2)}) collective-permute-start(f32[2,1024]{1,0:T(2,128)S(1)} %fusion.12), channel_id=1, source_target_pairs={{0,128},{128,0},{1,129},{129,1},{2,130},{130,2},{3,131},{131,3},{4... | collective-permute-start | bytes 24584 | tf_op jit(solution)/shard_map/ppermute | solution.py:65
  18.6 13.1 %all-to-all-start = ((f32[16,2,1024]{2,1,0:T(2,128)}), f32[16,2,1024]{2,1,0:T(2,128)S(1)}, u32[]{:S(2)}, u32[]{:S(2)}) async-start(f32[16,2,1024]{2,1,0:T(2,128)} %broadcast_in_dim.8), calls=%async_computation | async-start | bytes 262144 | tf_op jit(solution)/shard_map/all_to_all | solution.py:53
  26.4 8.1 %collective-permute-start.4 = (bf16[96,1024]{1,0:T(8,128)(2,1)S(1)}, bf16[96,1024]{1,0:T(8,128)(2,1)S(1)}, u32[]{:S(2)}, u32[]{:S(2)}) collective-permute-start(bf16[96,1024]{1,0:T(8,128)(2,1)S(1)} %get-tuple-element.48), channel_id=1, source_target_pairs={{0,96},{1,25},{8,104},{9,1},{16,112},{17,9},{24,120},{25,17},{32,0... | collective-permute-start | bytes 589832 | tf_op jit(solution)/shard_map/ppermute | solution.py:75
  29.1 7.3 %collective-permute-start.5 = (bf16[96,1024]{1,0:T(8,128)(2,1)S(1)}, bf16[96,1024]{1,0:T(8,128)(2,1)S(1)}, u32[]{:S(2)}, u32[]{:S(2)}) collective-permute-start(bf16[96,1024]{1,0:T(8,128)(2,1)S(1)} %get-tuple-element.48), channel_id=1, source_target_pairs={{0,64},{1,17},{8,72},{9,25},{16,80},{17,1},{24,88},{25,9},{32,96},... | collective-permute-start | bytes 589832 | tf_op jit(solution)/shard_map/ppermute | solution.py:75
  30.0 8.4 %collective-permute-start.6 = (bf16[96,1024]{1,0:T(8,128)(2,1)S(1)}, bf16[96,1024]{1,0:T(8,128)(2,1)S(1)}, u32[]{:S(2)}, u32[]{:S(2)}) collective-permute-start(bf16[96,1024]{1,0:T(8,128)(2,1)S(1)} %get-tuple-element.48), channel_id=1, source_target_pairs={{0,32},{1,9},{8,40},{9,17},{16,48},{17,25},{24,56},{25,1},{32,64},... | collective-permute-start | bytes 589832 | tf_op jit(solution)/shard_map/ppermute | solution.py:75
  33.8 9.7 %collective-permute-start.2 = (f32[3,512]{1,0:T(4,128)S(1)}, f32[3,512]{1,0:T(4,128)S(1)}, u32[]{:S(2)}, u32[]{:S(2)}) collective-permute-start(f32[3,512]{1,0:T(4,128)S(1)} %bitcast.86), channel_id=1, source_target_pairs={{0,1},{1,0},{2,3},{3,2},{4,5},{5,4},{6,7},{7,6},{8,9},{9,8},{10,11... | collective-permute-start | bytes 18440 | tf_op jit(solution)/shard_map/ppermute | solution.py:100
  39.4 21.9 %collective-permute-start.7 = (bf16[4,96,1024]{2,1,0:T(8,128)(2,1)}, bf16[4,96,1024]{2,1,0:T(8,128)(2,1)}, u32[]{:S(2)}, u32[]{:S(2)}) collective-permute-start(bf16[4,96,1024]{2,1,0:T(8,128)(2,1)} %pad_maximum_fusion.refs_0_), channel_id=1, source_target_pairs={{0,24},{1,97},{8,0},{9,105},{16,8},{17,113},{24,16},{25,121},{32,5... | collective-permute-start | bytes 2359304 | tf_op jit(solution)/shard_map/ppermute | solution.py:82
  40.2 21.1 %collective-permute-start.8 = (bf16[4,96,1024]{2,1,0:T(8,128)(2,1)}, bf16[4,96,1024]{2,1,0:T(8,128)(2,1)}, u32[]{:S(2)}, u32[]{:S(2)}) collective-permute-start(bf16[4,96,1024]{2,1,0:T(8,128)(2,1)} %pad_maximum_fusion.refs_0_), channel_id=1, source_target_pairs={{0,16},{1,65},{8,24},{9,73},{16,0},{17,81},{24,8},{25,89},{32,48},... | collective-permute-start | bytes 2359304 | tf_op jit(solution)/shard_map/ppermute | solution.py:82
  41.4 20.8 %collective-permute-start.9 = (bf16[4,96,1024]{2,1,0:T(8,128)(2,1)}, bf16[4,96,1024]{2,1,0:T(8,128)(2,1)}, u32[]{:S(2)}, u32[]{:S(2)}) collective-permute-start(bf16[4,96,1024]{2,1,0:T(8,128)(2,1)} %pad_maximum_fusion.refs_0_), channel_id=1, source_target_pairs={{0,8},{1,33},{8,16},{9,41},{16,24},{17,49},{24,0},{25,57},{32,40},... | collective-permute-start | bytes 2359304 | tf_op jit(solution)/shard_map/ppermute | solution.py:82
  44.1 15.5 %all-to-all-start.1 = ((f32[8,3,512]{2,1,0:T(4,128)}), f32[8,3,512]{2,1,0:T(4,128)S(1)}, u32[]{:S(2)}, u32[]{:S(2)}) async-start(f32[8,3,512]{2,1,0:T(4,128)} %broadcast_in_dim.9), calls=%async_computation.1 | async-start | bytes 131072 | tf_op jit(solution)/shard_map/all_to_all | solution.py:53
  77.5 11.2 %collective-permute-start.11 = (f32[128,768]{1,0:T(8,128)S(1)}, f32[128,768]{1,0:T(8,128)S(1)}, u32[]{:S(2)}, u32[]{:S(2)}) collective-permute-start(f32[128,768]{1,0:T(8,128)S(1)} %get-tuple-element.41), channel_id=1, source_target_pairs={{0,128},{128,0},{1,129},{129,1},{2,130},{130,2},{3,131},{131,3},{4... | collective-permute-start | bytes 1179656 | tf_op jit(solution)/shard_map/ppermute | solution.py:65
  78.5 12.0 %collective-permute-start.12 = (f32[128,768]{1,0:T(8,128)S(1)}, f32[128,768]{1,0:T(8,128)S(1)}, u32[]{:S(2)}, u32[]{:S(2)}) collective-permute-start(f32[128,768]{1,0:T(8,128)S(1)} %get-tuple-element.42), channel_id=1, source_target_pairs={{0,134},{2,128},{4,130},{6,132},{128,2},{130,4},{132,6},{134,0},{1... | collective-permute-start | bytes 1179656 | tf_op jit(solution)/shard_map/ppermute | solution.py:66
  90.7 8.8 %collective-permute-start.13 = (f32[16,1536]{1,0:T(8,128)S(1)}, f32[16,1536]{1,0:T(8,128)S(1)}, u32[]{:S(2)}, u32[]{:S(2)}) collective-permute-start(f32[16,1536]{1,0:T(8,128)S(1)} %get-tuple-element.11), channel_id=1, source_target_pairs={{0,2},{2,4},{4,6},{6,0},{1,3},{3,5},{5,7},{7,1},{8,10},{10,12},{12... | collective-permute-start | bytes 294920 | tf_op jit(solution)/shard_map/ppermute | solution.py:124
  94.3 5.6 %collective-permute-start.14 = (f32[16,1536]{1,0:T(8,128)S(1)}, f32[16,1536]{1,0:T(8,128)S(1)}, u32[]{:S(2)}, u32[]{:S(2)}) collective-permute-start(f32[16,1536]{1,0:T(8,128)S(1)} %get-tuple-element.12), channel_id=1, source_target_pairs={{2,0},{4,2},{6,4},{0,6},{3,1},{5,3},{7,5},{1,7},{10,8},{12,10},{14... | collective-permute-start | bytes 294920 | tf_op jit(solution)/shard_map/ppermute | solution.py:125
  100.0 12.1 %collective-permute-start.15 = (f32[32,1536]{1,0:T(8,128)S(1)}, f32[32,1536]{1,0:T(8,128)S(1)}, u32[]{:S(2)}, u32[]{:S(2)}) collective-permute-start(f32[32,1536]{1,0:T(8,128)S(1)} %get-tuple-element.15), channel_id=1, source_target_pairs={{0,2},{2,4},{4,6},{6,0},{1,3},{3,5},{5,7},{7,1},{8,10},{10,12},{12... | collective-permute-start | bytes 589832 | tf_op jit(solution)/shard_map/ppermute | solution.py:124
  104.2 10.7 %collective-permute-start.16 = (f32[32,1536]{1,0:T(8,128)S(1)}, f32[32,1536]{1,0:T(8,128)S(1)}, u32[]{:S(2)}, u32[]{:S(2)}) collective-permute-start(f32[32,1536]{1,0:T(8,128)S(1)} %get-tuple-element.16), channel_id=1, source_target_pairs={{2,0},{4,2},{6,4},{0,6},{3,1},{5,3},{7,5},{1,7},{10,8},{12,10},{14... | collective-permute-start | bytes 589832 | tf_op jit(solution)/shard_map/ppermute | solution.py:125
  130.0 5.8 %collective-permute-start.17 = (bf16[128,768]{1,0:T(8,128)(2,1)S(1)}, bf16[128,768]{1,0:T(8,128)(2,1)S(1)}, u32[]{:S(2)}, u32[]{:S(2)}) collective-permute-start(bf16[128,768]{1,0:T(8,128)(2,1)S(1)} %get-tuple-element.46), channel_id=1, source_target_pairs={{0,128},{128,0},{1,129},{129,1},{2,130},{130,2},{3,131},{131,3},{4... | collective-permute-start | bytes 589832 | tf_op jit(solution)/shard_map/ppermute | solution.py:65
  131.5 5.7 %collective-permute-start.18 = (bf16[128,768]{1,0:T(8,128)(2,1)S(1)}, bf16[128,768]{1,0:T(8,128)(2,1)S(1)}, u32[]{:S(2)}, u32[]{:S(2)}) collective-permute-start(bf16[128,768]{1,0:T(8,128)(2,1)S(1)} %get-tuple-element.45), channel_id=1, source_target_pairs={{0,134},{2,128},{4,130},{6,132},{128,2},{130,4},{132,6},{134,0},{1... | collective-permute-start | bytes 589832 | tf_op jit(solution)/shard_map/ppermute | solution.py:66
  137.3 6.4 %collective-permute-start.19 = (bf16[256,1536]{1,0:T(8,128)(2,1)S(1)}, bf16[256,1536]{1,0:T(8,128)(2,1)S(1)}, u32[]{:S(2)}, u32[]{:S(2)}) collective-permute-start(bf16[256,1536]{1,0:T(8,128)(2,1)S(1)} %maximum_select_fusion.2), channel_id=1, source_target_pairs={{0,1},{1,0},{2,3},{3,2},{4,5},{5,4},{6,7},{7,6},{8,9},{9,8},{10,11... | collective-permute-start | bytes 2359304 | tf_op jit(solution)/shard_map/ppermute | solution.py:153
  138.6 10.6 %all-to-all-start.4 = ((f32[16,1,96]{2,1,0:T(1,128)}), f32[16,1,96]{2,1,0:T(1,128)S(1)}, u32[]{:S(2)}, u32[]{:S(2)}) async-start(f32[16,1,96]{2,1,0:T(1,128)} %broadcast_in_dim.11), calls=%async_computation.4 | async-start | bytes 16384 | tf_op jit(solution)/shard_map/all_to_all | solution.py:53
  149.3 50.0 %all-to-all-start.3 = ((bf16[32,48,1024]{2,1,0:T(8,128)(2,1)}), bf16[32,48,1024]{2,1,0:T(8,128)(2,1)S(1)}, u32[]{:S(2)}, u32[]{:S(2)}) async-start(bf16[32,48,1024]{2,1,0:T(8,128)(2,1)} %bitcast.72), calls=%async_computation.3 | async-start | bytes 6291456 | tf_op jit(solution)/shard_map/all_to_all | solution.py:160
  157.2 36.6 %collective-permute-start.20 = (f32[1,96]{1,0:T(1,128)S(1)}, f32[1,96]{1,0:T(1,128)S(1)}, u32[]{:S(2)}, u32[]{:S(2)}) collective-permute-start(f32[1,96]{1,0:T(1,128)S(1)} %bitcast.92), channel_id=1, source_target_pairs={{0,128},{128,0},{1,129},{129,1},{2,130},{130,2},{3,131},{131,3},{4... | collective-permute-start | bytes 1160 | tf_op jit(solution)/shard_map/ppermute | solution.py:65
  (7 other events, 52.9 us)

commit v5 on v4

--- a/solution.py
+++ b/solution.py
@@ -25,7 +25,7 @@
 
 
 def put_kernel(at, *refs):
-    out = refs[4]
+    out, energy = refs[4], refs[5]
     zl, core, first, second = at[0], at[1], at[2], at[3]
     rows = out.shape[1]
     for t in range(4):
@@ -34,17 +34,26 @@
             p = (first + s) % 4
             spot = jnp.where(core == 0, p * 4 + q, q * 4 + p)
             for k in range(2):
-                out[(zl + k) % 2 * 16 + spot] = refs[t][s, k * rows : (k + 1) * rows]
+                piece = refs[t][s, k * rows : (k + 1) * rows]
+                index = (zl + k) % 2 * 16 + spot
+                out[index] = piece
+                square = jnp.square(piece.astype(F32))
+                energy[index] = sum(
+                    square[:, lane : lane + 128] for lane in range(0, square.shape[1], 128)
+                )
 
 
 def put_together(at, parts):
     vmem = pl.BlockSpec(memory_space=pltpu.VMEM)
-    shape = (32, parts[0].shape[1] // 2, parts[0].shape[2])
+    rows, pixels = parts[0].shape[1] // 2, parts[0].shape[2]
     return pl.pallas_call(
         put_kernel,
         in_specs=[pl.BlockSpec(memory_space=pltpu.SMEM)] + [vmem] * 4,
-        out_specs=vmem,
-        out_shape=jax.ShapeDtypeStruct(shape, parts[0].dtype),
+        out_specs=(vmem, vmem),
+        out_shape=(
+            jax.ShapeDtypeStruct((32, rows, pixels), parts[0].dtype),
+            jax.ShapeDtypeStruct((32, rows, 128), F32),
+        ),
     )(at, *parts)
 
 
@@ -107,20 +116,25 @@
     normed = ((whitened - bg_mean[:, None]) / bg_std[:, None]).astype(BF16)
 
     first, second = jnp.where(core == 0, x, y), jnp.where(core == 0, y, x)
-    refs = put_together(jnp.stack([zl, core, first, second]), sheet)
+    refs, energy = put_together(jnp.stack([zl, core, first, second]), sheet)
     refs = refs.reshape(32 * views, half)
-    ref_energy = jnp.sum(jnp.square(refs.astype(F32)), 1)
+    ref_energy = jnp.sum(energy, 2).reshape(-1)
     score = lambda a: (
         lax.dot_general(a, refs, (((1,), (1,)), ((), ())), preferred_element_type=F32)
         - 0.5 * ref_energy[None, :]
     )
-    both = lax.ppermute(score(normed[rows:]), "c", PAIR)
-    both = both + lax.optimization_barrier(score(normed[:rows]))
-    both = both.reshape(2, rows // 2, 32 * views)
+    theirs_part = lax.ppermute(score(normed[rows:]), "c", PAIR)
+    own_part = lax.optimization_barrier(score(normed[:rows]))
     cut = 16 * views
-    kept = lax.dynamic_index_in_dim(both, zl, 0, False)
-    sent = lax.dynamic_index_in_dim(both, 1 - zl, 0, False)
-    kept = kept + jnp.concatenate([swap(sent[:, :cut]), far(sent[:, cut:])], 1)
+    deep = rows // 2
+
+    def added(place, start, count):
+        at, size = (place * deep, start), (deep, count)
+        return lax.dynamic_slice(theirs_part, at, size) + lax.dynamic_slice(own_part, at, size)
+
+    leaving = lax.optimization_barrier((added(1 - zl, 0, cut), added(1 - zl, cut, cut)))
+    came = jnp.concatenate([swap(leaving[0]), far(leaving[1])], 1)
+    kept = added(zl, 0, 2 * cut) + came
     up = lambda a: lax.ppermute(a, "zh", [(i, (i + 1) % 4) for i in range(4)])
     down = lambda a: lax.ppermute(a, "zh", [((i + 1) % 4, i) for i in range(4)])
     take = lambda step, skip, count: lax.dynamic_slice_in_dim(

time: 201 us -> 190 us (0.945)
  the two profiles are of different devices: /device:TPU:56 before, /device:TPU:34 now
where the time goes in v5:
time: 190 us; the launch traced here: 189 us
  waiting for transfers between devices  83.1 us (44%)
  starting transfers between devices  59.7 us (31%)
  blocking collectives  13.3 us (7%)
  other arithmetic  11.7 us (6%)
  matrix products  11.1 us (6%)
  local copies, waits for them, and re-layouts  4.88 us (3%)
  Pallas kernels  4.69 us (2%)
    ppermute x6, waiting for transfers between devices, on_device(): swap = lambda a: lax.ppermute(a, 'zl', PAIR)  46.9 us
    all_to_all x3, starting transfers between devices, spread(): return lax.all_to_all(sent, axes, split_axis=0, concat_axis=0)  24.2 us
    all_to_all x1, blocking collectives, spread(): return lax.all_to_all(sent, axes, split_axis=0, concat_axis=0)  13.3 us
    all_to_all x3, waiting for transfers between devices, spread(): return lax.all_to_all(sent, axes, split_axis=0, concat_axis=0)  10.9 us
    ppermute x2, waiting for transfers between devices, on_device(): up = lambda a: lax.ppermute(a, 'zh', [(i, (i + 1) % 4) for i in range(4)])  10.7 us
    ppermute x2, starting transfers between devices, on_device(): up = lambda a: lax.ppermute(a, 'zh', [(i, (i + 1) % 4) for i in range(4)])  8.64 us
    dot_general x2, matrix products, on_device(): lax.dot_general(a, refs, (((1,), (1,)), ((), ())), preferred_element_type...  7.14 us
    ppermute x6, starting transfers between devices, on_device(): swap = lambda a: lax.ppermute(a, 'zl', PAIR)  6.87 us
  transfers between devices with their start and end apart: 26, of which 15 were waited for; matrix products, arithmetic and copies ran while one was open for 8% of the time, Pallas kernels for 0%

profile of v5, /device:TPU:34, one launch (start us, length us, event | category | flops | bytes accessed | tf_op | source)
XLA Modules:
  0.0 189.4 jit_solution(8214968195329808774)
XLA Ops:
  7.2 7.5 %all-to-all-start = ((f32[16,2,1024]{2,1,0:T(2,128)}), f32[16,2,1024]{2,1,0:T(2,128)S(1)}, u32[]{:S(2)}, u32[]{:S(2)}) async-start(f32[16,2,1024]{2,1,0:T(2,128)} %broadcast_in_dim.8), calls=%async_computation | async-start | bytes 262144 | tf_op jit(solution)/shard_map/all_to_all | solution.py:62
  15.4 2.2 %collective-permute-start.5 = (bf16[96,1024]{1,0:T(8,128)(2,1)S(1)}, bf16[96,1024]{1,0:T(8,128)(2,1)S(1)}, u32[]{:S(2)}, u32[]{:S(2)}) collective-permute-start(bf16[96,1024]{1,0:T(8,128)(2,1)S(1)} %get-tuple-element.56), channel_id=1, source_target_pairs={{0,64},{1,17},{8,72},{9,25},{16,80},{17,1},{24,88},{25,9},{32,96},... | collective-permute-start | bytes 589832 | tf_op jit(solution)/shard_map/ppermute | solution.py:84
  27.2 2.7 %collective-permute-start.8 = (bf16[4,96,1024]{2,1,0:T(8,128)(2,1)}, bf16[4,96,1024]{2,1,0:T(8,128)(2,1)}, u32[]{:S(2)}, u32[]{:S(2)}) collective-permute-start(bf16[4,96,1024]{2,1,0:T(8,128)(2,1)} %pad_maximum_fusion.refs_0_), channel_id=1, source_target_pairs={{0,16},{1,65},{8,24},{9,73},{16,0},{17,81},{24,8},{25,89},{32,48},... | collective-permute-start | bytes 2359304 | tf_op jit(solution)/shard_map/ppermute | solution.py:91
  32.0 9.5 %all-to-all-start.1 = ((f32[8,3,512]{2,1,0:T(4,128)}), f32[8,3,512]{2,1,0:T(4,128)S(1)}, u32[]{:S(2)}, u32[]{:S(2)}) async-start(f32[8,3,512]{2,1,0:T(4,128)} %broadcast_in_dim.9), calls=%async_computation.1 | async-start | bytes 131072 | tf_op jit(solution)/shard_map/all_to_all | solution.py:62
  41.7 6.7 %all-to-all-done.1 = f32[8,3,512]{2,1,0:T(4,128)S(1)} async-done(((f32[8,3,512]{2,1,0:T(4,128)}), f32[8,3,512]{2,1,0:T(4,128)S(1)}, u32[]{:S(2)}, u32[]{:S(2)}) %all-to-all-start.1) | async-done | bytes 49184 | tf_op jit(solution)/shard_map/all_to_all | solution.py:62
  49.0 4.7 %shard_map.67 = (bf16[32,48,1024]{2,1,0:T(8,128)(2,1)}, f32[32,48,128]{2,1,0:T(8,128)}) custom-call(s32[4]{0:T(128)} %pad_add_fusion.at, bf16[4,96,1024]{2,1,0:T(8,128)(2,1)} %pad_maximum_fusion.refs_0_, bf16[4,96,1024]{2,1,0:T(8,128)(2,1)} %collective-permute-done.7.refs_1_, bf16[4,96,1024]{2,1,0:T(8,128)(2,1)} %collective-permute-done.8.refs_2_, ...), custom_call_target="tpu_custom_call" | custom-call | tf_op jit(solution)/shard_map/pallas_call | solution.py:49
  55.2 4.1 %convolution_subtract_fusion.1 = f32[256,1536]{1,0:T(8,128)} fusion(bf16[1536,1024]{1,0:T(8,128)(2,1)} %bitcast.84, f32[1536]{0:T(1024)S(1)} %mul.104, bf16[512,1024]{1,0:T(8,128)(2,1)S(1)} %fusion.4), kind=kOutput, calls=%fused_computation.3 | convolution fusion | flops 805699584 | bytes 5251072 | tf_op jit(solution)/shard_map/dot_general | solution.py:123
  59.2 3.1 %convolution_subtract_fusion = f32[256,1536]{1,0:T(8,128)S(1)} fusion(bf16[1536,1024]{1,0:T(8,128)(2,1)} %bitcast.85, f32[1536]{0:T(1024)S(1)} %mul.104, bf16[512,1024]{1,0:T(8,128)(2,1)} %copy-done.2), kind=kOutput, calls=%fused_computation.2 | convolution fusion | flops 805699584 | bytes 5249024 | tf_op jit(solution)/shard_map/dot_general | solution.py:123
  66.8 8.4 %collective-permute-done.11 = f32[128,768]{1,0:T(8,128)S(1)} collective-permute-done((f32[128,768]{1,0:T(8,128)S(1)}, f32[128,768]{1,0:T(8,128)S(1)}, u32[]{:S(2)}, u32[]{:S(2)}) %collective-permute-start.11) | collective-permute-done | bytes 393248 | tf_op jit(solution)/shard_map/ppermute | solution.py:74
  77.9 4.3 %collective-permute-start.13 = (f32[16,1536]{1,0:T(8,128)S(1)}, f32[16,1536]{1,0:T(8,128)S(1)}, u32[]{:S(2)}, u32[]{:S(2)}) collective-permute-start(f32[16,1536]{1,0:T(8,128)S(1)} %get-tuple-element.19), channel_id=1, source_target_pairs={{0,2},{2,4},{4,6},{6,0},{1,3},{3,5},{5,7},{7,1},{8,10},{10,12},{12... | collective-permute-start | bytes 294920 | tf_op jit(solution)/shard_map/ppermute | solution.py:138
  82.1 2.0 %collective-permute-start.14 = (f32[16,1536]{1,0:T(8,128)S(1)}, f32[16,1536]{1,0:T(8,128)S(1)}, u32[]{:S(2)}, u32[]{:S(2)}) collective-permute-start(f32[16,1536]{1,0:T(8,128)S(1)} %get-tuple-element.20), channel_id=1, source_target_pairs={{2,0},{4,2},{6,4},{0,6},{3,1},{5,3},{7,5},{1,7},{10,8},{12,10},{14... | collective-permute-start | bytes 294920 | tf_op jit(solution)/shard_map/ppermute | solution.py:139
  84.2 3.6 %collective-permute-done.13 = f32[16,1536]{1,0:T(8,128)S(1)} collective-permute-done((f32[16,1536]{1,0:T(8,128)S(1)}, f32[16,1536]{1,0:T(8,128)S(1)}, u32[]{:S(2)}, u32[]{:S(2)}) %collective-permute-start.13) | collective-permute-done | bytes 98336 | tf_op jit(solution)/shard_map/ppermute | solution.py:138
  87.8 4.4 %collective-permute-start.15 = (f32[32,1536]{1,0:T(8,128)S(1)}, f32[32,1536]{1,0:T(8,128)S(1)}, u32[]{:S(2)}, u32[]{:S(2)}) collective-permute-start(f32[32,1536]{1,0:T(8,128)S(1)} %get-tuple-element.23), channel_id=1, source_target_pairs={{0,2},{2,4},{4,6},{6,0},{1,3},{3,5},{5,7},{7,1},{8,10},{10,12},{12... | collective-permute-start | bytes 589832 | tf_op jit(solution)/shard_map/ppermute | solution.py:138
  92.2 7.1 %collective-permute-done.15 = f32[32,1536]{1,0:T(8,128)S(1)} collective-permute-done((f32[32,1536]{1,0:T(8,128)S(1)}, f32[32,1536]{1,0:T(8,128)S(1)}, u32[]{:S(2)}, u32[]{:S(2)}) %collective-permute-start.15) | collective-permute-done | bytes 196640 | tf_op jit(solution)/shard_map/ppermute | solution.py:138
  99.3 3.9 %collective-permute-done.16 = f32[32,1536]{1,0:T(8,128)S(1)} collective-permute-done((f32[32,1536]{1,0:T(8,128)S(1)}, f32[32,1536]{1,0:T(8,128)S(1)}, u32[]{:S(2)}, u32[]{:S(2)}) %collective-permute-start.16) | collective-permute-done | bytes 196640 | tf_op jit(solution)/shard_map/ppermute | solution.py:139
  104.2 13.3 %all_to_all.25 = bf16[4,32,1536]{2,1,0:T(8,128)(2,1)S(1)} all-to-all(bf16[4,32,1536]{2,1,0:T(8,128)(2,1)S(1)} %broadcast_in_dim.10), channel_id=1, replica_groups=mesh['zl'=2,'x'=4,'y'=4,'zh'=4,'c'=2] {'zh'}, dimensions={0} | all-to-all | bytes 786432 | tf_op jit(solution)/shard_map/all_to_all | solution.py:62
  117.5 2.7 %collective-permute-start.17 = (bf16[128,768]{1,0:T(8,128)(2,1)S(1)}, bf16[128,768]{1,0:T(8,128)(2,1)S(1)}, u32[]{:S(2)}, u32[]{:S(2)}) collective-permute-start(bf16[128,768]{1,0:T(8,128)(2,1)S(1)} %get-tuple-element.54), channel_id=1, source_target_pairs={{0,128},{128,0},{1,129},{129,1},{2,130},{130,2},{3,131},{131,3},{4... | collective-permute-start | bytes 589832 | tf_op jit(solution)/shard_map/ppermute | solution.py:74
  120.2 3.6 %collective-permute-done.17 = bf16[128,768]{1,0:T(8,128)(2,1)S(1)} collective-permute-done((bf16[128,768]{1,0:T(8,128)(2,1)S(1)}, bf16[128,768]{1,0:T(8,128)(2,1)S(1)}, u32[]{:S(2)}, u32[]{:S(2)}) %collective-permute-start.17) | collective-permute-done | bytes 196640 | tf_op jit(solution)/shard_map/ppermute | solution.py:74
  127.4 7.2 %all-to-all-start.4 = ((f32[16,1,96]{2,1,0:T(1,128)}), f32[16,1,96]{2,1,0:T(1,128)S(1)}, u32[]{:S(2)}, u32[]{:S(2)}) async-start(f32[16,1,96]{2,1,0:T(1,128)} %broadcast_in_dim.11), calls=%async_computation.4 | async-start | bytes 16384 | tf_op jit(solution)/shard_map/all_to_all | solution.py:62
  134.6 3.5 %convolution_convert_fusion = bf16[1536,1024]{1,0:T(8,128)(2,1)} fusion(bf16[512,1024]{1,0:T(8,128)(2,1)S(1)} %copy-done.3, bf16[256,1536]{1,0:T(8,128)(2,1)S(1)} %collective-permute-done.19, bf16[256,1536]{1,0:T(8,128)(2,1)S(1)} %maximum_select_fusion.2), kind=kOutput, calls=%fused_computation.1 | convolution fusion | flops 1615331328 | bytes 5767168 | tf_op jit(solution)/shard_map/dot_general | solution.py:172
  138.0 2.7 %all-to-all-done.4 = f32[16,1,96]{2,1,0:T(1,128)S(1)} async-done(((f32[16,1,96]{2,1,0:T(1,128)}), f32[16,1,96]{2,1,0:T(1,128)S(1)}, u32[]{:S(2)}, u32[]{:S(2)}) %all-to-all-start.4) | async-done | bytes 6176 | tf_op jit(solution)/shard_map/all_to_all | solution.py:62
  140.7 6.1 %all-to-all-start.3 = ((bf16[32,48,1024]{2,1,0:T(8,128)(2,1)}), bf16[32,48,1024]{2,1,0:T(8,128)(2,1)S(1)}, u32[]{:S(2)}, u32[]{:S(2)}) async-start(bf16[32,48,1024]{2,1,0:T(8,128)(2,1)} %bitcast.63), calls=%async_computation.3 | async-start | bytes 6291456 | tf_op jit(solution)/shard_map/all_to_all | solution.py:174
  147.3 34.8 %collective-permute-done.20 = f32[1,96]{1,0:T(1,128)S(1)} collective-permute-done((f32[1,96]{1,0:T(1,128)S(1)}, f32[1,96]{1,0:T(1,128)S(1)}, u32[]{:S(2)}, u32[]{:S(2)}) %collective-permute-start.20) | collective-permute-done | bytes 416 | tf_op jit(solution)/shard_map/ppermute | solution.py:74
  183.8 4.1 %all-to-all-done.3 = bf16[32,48,1024]{2,1,0:T(8,128)(2,1)S(1)} async-done(((bf16[32,48,1024]{2,1,0:T(8,128)(2,1)}), bf16[32,48,1024]{2,1,0:T(8,128)(2,1)S(1)}, u32[]{:S(2)}, u32[]{:S(2)}) %all-to-all-start.3) | async-done | bytes 3145760 | tf_op jit(solution)/shard_map/all_to_all | solution.py:174
  (107 shorter events, 36.4 us)
Async XLA Ops:
  2.4 4.0 %collective-permute-start.1 = (f32[2,1024]{1,0:T(2,128)S(1)}, f32[2,1024]{1,0:T(2,128)S(1)}, u32[]{:S(2)}, u32[]{:S(2)}) collective-permute-start(f32[2,1024]{1,0:T(2,128)S(1)} %fusion.12), channel_id=1, source_target_pairs={{0,128},{128,0},{1,129},{129,1},{2,130},{130,2},{3,131},{131,3},{4... | collective-permute-start | bytes 24584 | tf_op jit(solution)/shard_map/ppermute | solution.py:74
  3.5 11.8 %collective-permute-start.3 = (bf16[48,1024]{1,0:T(8,128)(2,1)S(1)}, bf16[48,1024]{1,0:T(8,128)(2,1)S(1)}, u32[]{:S(2)}, u32[]{:S(2)}) collective-permute-start(bf16[48,1024]{1,0:T(8,128)(2,1)S(1)} %get-tuple-element.58), channel_id=1, source_target_pairs={{0,128},{128,0},{1,129},{129,1},{2,130},{130,2},{3,131},{131,3},{4... | collective-permute-start | bytes 294920 | tf_op jit(solution)/shard_map/ppermute | solution.py:74
  5.6 15.6 %collective-permute-start = (bf16[256,1024]{1,0:T(8,128)(2,1)S(1)}, bf16[256,1024]{1,0:T(8,128)(2,1)S(1)}, u32[]{:S(2)}, u32[]{:S(2)}) collective-permute-start(bf16[256,1024]{1,0:T(8,128)(2,1)S(1)} %get-tuple-element.44), channel_id=1, source_target_pairs={{0,128},{128,0},{1,129},{129,1},{2,130},{130,2},{3,131},{131,3},{4... | collective-permute-start | bytes 1572872 | tf_op jit(solution)/shard_map/ppermute | solution.py:74
  7.2 13.9 %all-to-all-start = ((f32[16,2,1024]{2,1,0:T(2,128)}), f32[16,2,1024]{2,1,0:T(2,128)S(1)}, u32[]{:S(2)}, u32[]{:S(2)}) async-start(f32[16,2,1024]{2,1,0:T(2,128)} %broadcast_in_dim.8), calls=%async_computation | async-start | bytes 262144 | tf_op jit(solution)/shard_map/all_to_all | solution.py:62
  15.4 7.9 %collective-permute-start.5 = (bf16[96,1024]{1,0:T(8,128)(2,1)S(1)}, bf16[96,1024]{1,0:T(8,128)(2,1)S(1)}, u32[]{:S(2)}, u32[]{:S(2)}) collective-permute-start(bf16[96,1024]{1,0:T(8,128)(2,1)S(1)} %get-tuple-element.56), channel_id=1, source_target_pairs={{0,64},{1,17},{8,72},{9,25},{16,80},{17,1},{24,88},{25,9},{32,96},... | collective-permute-start | bytes 589832 | tf_op jit(solution)/shard_map/ppermute | solution.py:84
  17.5 7.2 %collective-permute-start.4 = (bf16[96,1024]{1,0:T(8,128)(2,1)S(1)}, bf16[96,1024]{1,0:T(8,128)(2,1)S(1)}, u32[]{:S(2)}, u32[]{:S(2)}) collective-permute-start(bf16[96,1024]{1,0:T(8,128)(2,1)S(1)} %get-tuple-element.56), channel_id=1, source_target_pairs={{0,96},{1,25},{8,104},{9,1},{16,112},{17,9},{24,120},{25,17},{32,0... | collective-permute-start | bytes 589832 | tf_op jit(solution)/shard_map/ppermute | solution.py:84
  19.0 5.8 %collective-permute-start.6 = (bf16[96,1024]{1,0:T(8,128)(2,1)S(1)}, bf16[96,1024]{1,0:T(8,128)(2,1)S(1)}, u32[]{:S(2)}, u32[]{:S(2)}) collective-permute-start(bf16[96,1024]{1,0:T(8,128)(2,1)S(1)} %get-tuple-element.56), channel_id=1, source_target_pairs={{0,32},{1,9},{8,40},{9,17},{16,48},{17,25},{24,56},{25,1},{32,64},... | collective-permute-start | bytes 589832 | tf_op jit(solution)/shard_map/ppermute | solution.py:84
  23.1 8.2 %collective-permute-start.2 = (f32[3,512]{1,0:T(4,128)S(1)}, f32[3,512]{1,0:T(4,128)S(1)}, u32[]{:S(2)}, u32[]{:S(2)}) collective-permute-start(f32[3,512]{1,0:T(4,128)S(1)} %bitcast.77), channel_id=1, source_target_pairs={{0,1},{1,0},{2,3},{3,2},{4,5},{5,4},{6,7},{7,6},{8,9},{9,8},{10,11... | collective-permute-start | bytes 18440 | tf_op jit(solution)/shard_map/ppermute | solution.py:109
  25.7 23.2 %collective-permute-start.9 = (bf16[4,96,1024]{2,1,0:T(8,128)(2,1)}, bf16[4,96,1024]{2,1,0:T(8,128)(2,1)}, u32[]{:S(2)}, u32[]{:S(2)}) collective-permute-start(bf16[4,96,1024]{2,1,0:T(8,128)(2,1)} %pad_maximum_fusion.refs_0_), channel_id=1, source_target_pairs={{0,8},{1,33},{8,16},{9,41},{16,24},{17,49},{24,0},{25,57},{32,40},... | collective-permute-start | bytes 2359304 | tf_op jit(solution)/shard_map/ppermute | solution.py:91
  27.2 21.8 %collective-permute-start.8 = (bf16[4,96,1024]{2,1,0:T(8,128)(2,1)}, bf16[4,96,1024]{2,1,0:T(8,128)(2,1)}, u32[]{:S(2)}, u32[]{:S(2)}) collective-permute-start(bf16[4,96,1024]{2,1,0:T(8,128)(2,1)} %pad_maximum_fusion.refs_0_), channel_id=1, source_target_pairs={{0,16},{1,65},{8,24},{9,73},{16,0},{17,81},{24,8},{25,89},{32,48},... | collective-permute-start | bytes 2359304 | tf_op jit(solution)/shard_map/ppermute | solution.py:91
  29.9 19.1 %collective-permute-start.7 = (bf16[4,96,1024]{2,1,0:T(8,128)(2,1)}, bf16[4,96,1024]{2,1,0:T(8,128)(2,1)}, u32[]{:S(2)}, u32[]{:S(2)}) collective-permute-start(bf16[4,96,1024]{2,1,0:T(8,128)(2,1)} %pad_maximum_fusion.refs_0_), channel_id=1, source_target_pairs={{0,24},{1,97},{8,0},{9,105},{16,8},{17,113},{24,16},{25,121},{32,5... | collective-permute-start | bytes 2359304 | tf_op jit(solution)/shard_map/ppermute | solution.py:91
  32.0 16.4 %all-to-all-start.1 = ((f32[8,3,512]{2,1,0:T(4,128)}), f32[8,3,512]{2,1,0:T(4,128)S(1)}, u32[]{:S(2)}, u32[]{:S(2)}) async-start(f32[8,3,512]{2,1,0:T(4,128)} %broadcast_in_dim.9), calls=%async_computation.1 | async-start | bytes 131072 | tf_op jit(solution)/shard_map/all_to_all | solution.py:62
  63.6 11.6 %collective-permute-start.11 = (f32[128,768]{1,0:T(8,128)S(1)}, f32[128,768]{1,0:T(8,128)S(1)}, u32[]{:S(2)}, u32[]{:S(2)}) collective-permute-start(f32[128,768]{1,0:T(8,128)S(1)} %get-tuple-element.17), channel_id=1, source_target_pairs={{0,128},{128,0},{1,129},{129,1},{2,130},{130,2},{3,131},{131,3},{4... | collective-permute-start | bytes 1179656 | tf_op jit(solution)/shard_map/ppermute | solution.py:74
  64.9 11.7 %collective-permute-start.12 = (f32[128,768]{1,0:T(8,128)S(1)}, f32[128,768]{1,0:T(8,128)S(1)}, u32[]{:S(2)}, u32[]{:S(2)}) collective-permute-start(f32[128,768]{1,0:T(8,128)S(1)} %get-tuple-element.18), channel_id=1, source_target_pairs={{0,134},{2,128},{4,130},{6,132},{128,2},{130,4},{132,6},{134,0},{1... | collective-permute-start | bytes 1179656 | tf_op jit(solution)/shard_map/ppermute | solution.py:75
  77.9 9.9 %collective-permute-start.13 = (f32[16,1536]{1,0:T(8,128)S(1)}, f32[16,1536]{1,0:T(8,128)S(1)}, u32[]{:S(2)}, u32[]{:S(2)}) collective-permute-start(f32[16,1536]{1,0:T(8,128)S(1)} %get-tuple-element.19), channel_id=1, source_target_pairs={{0,2},{2,4},{4,6},{6,0},{1,3},{3,5},{5,7},{7,1},{8,10},{10,12},{12... | collective-permute-start | bytes 294920 | tf_op jit(solution)/shard_map/ppermute | solution.py:138
  82.1 5.6 %collective-permute-start.14 = (f32[16,1536]{1,0:T(8,128)S(1)}, f32[16,1536]{1,0:T(8,128)S(1)}, u32[]{:S(2)}, u32[]{:S(2)}) collective-permute-start(f32[16,1536]{1,0:T(8,128)S(1)} %get-tuple-element.20), channel_id=1, source_target_pairs={{2,0},{4,2},{6,4},{0,6},{3,1},{5,3},{7,5},{1,7},{10,8},{12,10},{14... | collective-permute-start | bytes 294920 | tf_op jit(solution)/shard_map/ppermute | solution.py:139
  87.8 11.5 %collective-permute-start.15 = (f32[32,1536]{1,0:T(8,128)S(1)}, f32[32,1536]{1,0:T(8,128)S(1)}, u32[]{:S(2)}, u32[]{:S(2)}) collective-permute-start(f32[32,1536]{1,0:T(8,128)S(1)} %get-tuple-element.23), channel_id=1, source_target_pairs={{0,2},{2,4},{4,6},{6,0},{1,3},{3,5},{5,7},{7,1},{8,10},{10,12},{12... | collective-permute-start | bytes 589832 | tf_op jit(solution)/shard_map/ppermute | solution.py:138
  92.2 11.0 %collective-permute-start.16 = (f32[32,1536]{1,0:T(8,128)S(1)}, f32[32,1536]{1,0:T(8,128)S(1)}, u32[]{:S(2)}, u32[]{:S(2)}) collective-permute-start(f32[32,1536]{1,0:T(8,128)S(1)} %get-tuple-element.24), channel_id=1, source_target_pairs={{2,0},{4,2},{6,4},{0,6},{3,1},{5,3},{7,5},{1,7},{10,8},{12,10},{14... | collective-permute-start | bytes 589832 | tf_op jit(solution)/shard_map/ppermute | solution.py:139
  117.5 6.4 %collective-permute-start.17 = (bf16[128,768]{1,0:T(8,128)(2,1)S(1)}, bf16[128,768]{1,0:T(8,128)(2,1)S(1)}, u32[]{:S(2)}, u32[]{:S(2)}) collective-permute-start(bf16[128,768]{1,0:T(8,128)(2,1)S(1)} %get-tuple-element.54), channel_id=1, source_target_pairs={{0,128},{128,0},{1,129},{129,1},{2,130},{130,2},{3,131},{131,3},{4... | collective-permute-start | bytes 589832 | tf_op jit(solution)/shard_map/ppermute | solution.py:74
  120.2 5.7 %collective-permute-start.18 = (bf16[128,768]{1,0:T(8,128)(2,1)S(1)}, bf16[128,768]{1,0:T(8,128)(2,1)S(1)}, u32[]{:S(2)}, u32[]{:S(2)}) collective-permute-start(bf16[128,768]{1,0:T(8,128)(2,1)S(1)} %get-tuple-element.53), channel_id=1, source_target_pairs={{0,134},{2,128},{4,130},{6,132},{128,2},{130,4},{132,6},{134,0},{1... | collective-permute-start | bytes 589832 | tf_op jit(solution)/shard_map/ppermute | solution.py:75
  126.1 8.5 %collective-permute-start.19 = (bf16[256,1536]{1,0:T(8,128)(2,1)S(1)}, bf16[256,1536]{1,0:T(8,128)(2,1)S(1)}, u32[]{:S(2)}, u32[]{:S(2)}) collective-permute-start(bf16[256,1536]{1,0:T(8,128)(2,1)S(1)} %maximum_select_fusion.2), channel_id=1, source_target_pairs={{0,1},{1,0},{2,3},{3,2},{4,5},{5,4},{6,7},{7,6},{8,9},{9,8},{10,11... | collective-permute-start | bytes 2359304 | tf_op jit(solution)/shard_map/ppermute | solution.py:167
  127.4 13.3 %all-to-all-start.4 = ((f32[16,1,96]{2,1,0:T(1,128)}), f32[16,1,96]{2,1,0:T(1,128)S(1)}, u32[]{:S(2)}, u32[]{:S(2)}) async-start(f32[16,1,96]{2,1,0:T(1,128)} %broadcast_in_dim.11), calls=%async_computation.4 | async-start | bytes 16384 | tf_op jit(solution)/shard_map/all_to_all | solution.py:62
  140.7 47.3 %all-to-all-start.3 = ((bf16[32,48,1024]{2,1,0:T(8,128)(2,1)}), bf16[32,48,1024]{2,1,0:T(8,128)(2,1)S(1)}, u32[]{:S(2)}, u32[]{:S(2)}) async-start(bf16[32,48,1024]{2,1,0:T(8,128)(2,1)} %bitcast.63), calls=%async_computation.3 | async-start | bytes 6291456 | tf_op jit(solution)/shard_map/all_to_all | solution.py:174
  146.8 35.4 %collective-permute-start.20 = (f32[1,96]{1,0:T(1,128)S(1)}, f32[1,96]{1,0:T(1,128)S(1)}, u32[]{:S(2)}, u32[]{:S(2)}) collective-permute-start(f32[1,96]{1,0:T(1,128)S(1)} %bitcast.83), channel_id=1, source_target_pairs={{0,128},{128,0},{1,129},{129,1},{2,130},{130,2},{3,131},{131,3},{4... | collective-permute-start | bytes 1160 | tf_op jit(solution)/shard_map/ppermute | solution.py:74
  (8 other events, 61.4 us)
